TPU v7x, 32 devices: a whole 2x2x4 slice. The times are simulated.
32 devices in a mesh: batch: 8 (over z, y), dim: 4 (over x, core).
Axes of the slice: x: 2, y: 2, z: 4, core: 2. Of those that a mesh axis runs over, the one named last changes fastest.
Arguments:
- x_start: float32 [1024], P('dim'), may hold values from 0.5 to 2
- y_start: float32 [], replicated, may hold values from -1 to 1
- z_start: float32 [1024], P('dim'), may hold values from -3 to 3
- increments: float32 [5, 2048, 1024], P(None, 'batch', 'dim'), may hold values from -2.7 to 2.7
- default_step: int32 [2048], P('batch'), may hold values from 0 to 6
- term_weight: float32 [1024], P('dim'), may hold values from -6 to 6
- w_first: bfloat16 [4, 1024, 1024], P(None, None, 'dim'), may hold values from -0.1875 to 0.1875
- w_second: bfloat16 [4, 1024, 1024], P(None, 'dim'), may hold values from -0.1875 to 0.1875
- w_third: bfloat16 [4, 1024, 1024], P(None, None, 'dim'), may hold values from -0.1875 to 0.1875
Outputs:
- loss: float32 [], replicated
- grad_y: float32 [], replicated
- grad_z: float32 [1024], P('dim')
- grad_first: bfloat16 [4, 1024, 1024], P(None, None, 'dim')
- grad_second: bfloat16 [4, 1024, 1024], P(None, 'dim')
- grad_third: bfloat16 [4, 1024, 1024], P(None, None, 'dim')
Inputs may be any that keep to these rules, and one draw needn't show every extreme that they name: `default_step`: the time step at which a path defaults; 5 or more means no default within the window.
All inputs are finite; a program needn't handle non-finite values.
Results may differ from a plain program's by a relative error of at most 0.0085.
Values may be sent and summed in bfloat16 or wider, within the bound.
A program may use at most 64 MiB of HBM per device.

v0:
```python
import math

import jax
import jax.numpy as jnp
from jax import lax
from jax.sharding import PartitionSpec as P

D = 1024


DRIFT_RATE = 0.06
VOLATILITY = 0.2
DISCOUNT = 0.02
DEFAULT_LOSS = 1.0 / 3.0


def local(
    x_start, y_start, z_start, increments, default_step, term_weight, w_first, w_second, w_third
):
    steps = increments.shape[0]
    tstep = 1.0 / steps
    local_paths = increments.shape[1]
    scale = 1.0 / math.sqrt(local_paths * lax.axis_size("batch"))
    counter = jnp.arange(steps, dtype=jnp.int32)
    factors = (
        1.0
        + DISCOUNT * tstep
        - DEFAULT_LOSS * (counter[:, None] == default_step[None, :]).astype(jnp.float32)
    )
    states = jnp.broadcast_to(x_start[None, :], (local_paths, x_start.shape[0]))
    partials = [jnp.sum(increments[0] * z_start[None, :], axis=1)]
    states = states * (1.0 + DRIFT_RATE * tstep + VOLATILITY * increments[0])
    saved = []
    for index in range(1, steps):
        inputs_bf = lax.all_gather(states.astype(jnp.bfloat16), "dim", axis=1, tiled=True)
        tanh_first = jnp.tanh(
            jnp.dot(inputs_bf, w_first[index - 1], preferred_element_type=jnp.float32)
        )
        hidden_first = tanh_first.astype(jnp.bfloat16)
        part_second = jnp.dot(hidden_first, w_second[index - 1], preferred_element_type=jnp.float32)
        tanh_second = jnp.tanh(
            lax.psum_scatter(part_second, "dim", scatter_dimension=1, tiled=True)
        )
        hidden_second = lax.all_gather(tanh_second.astype(jnp.bfloat16), "dim", axis=1, tiled=True)
        control = jnp.dot(hidden_second, w_third[index - 1], preferred_element_type=jnp.float32)
        partials.append(jnp.sum(control * increments[index], axis=1))
        saved.append((inputs_bf, tanh_first, hidden_first, tanh_second, hidden_second))
        states = states * (1.0 + DRIFT_RATE * tstep + VOLATILITY * increments[index])
    target_part = jnp.sum(states * term_weight[None, :], axis=1) / math.sqrt(D)
    value = jnp.broadcast_to(y_start, (local_paths,))
    for index in range(steps):
        value = factors[index] * value + lax.psum(partials[index], "dim")
    target = lax.psum(target_part, "dim")
    error = value - target
    loss_local = scale * jnp.sum(error * error)
    adjoint = 2.0 * scale * error
    firsts, seconds, thirds = ([], [], [])
    for index in range(steps - 1, 0, -1):
        inputs_bf, tanh_first, hidden_first, tanh_second, hidden_second = saved[index - 1]
        d_control = (adjoint[:, None] * increments[index]).astype(jnp.bfloat16)
        grad_out = jnp.dot(hidden_second.T, d_control, preferred_element_type=jnp.float32)
        back_part = jnp.dot(d_control, w_third[index - 1].T, preferred_element_type=jnp.float32)
        back_share = lax.psum_scatter(back_part, "dim", scatter_dimension=1, tiled=True)
        d_share = (back_share * (1.0 - tanh_second * tanh_second)).astype(jnp.bfloat16)
        d_second = lax.all_gather(d_share, "dim", axis=1, tiled=True)
        grad_mid = jnp.dot(hidden_first.T, d_second, preferred_element_type=jnp.float32)
        back_first = jnp.dot(d_second, w_second[index - 1].T, preferred_element_type=jnp.float32)
        d_first = (back_first * (1.0 - tanh_first * tanh_first)).astype(jnp.bfloat16)
        grad_in = jnp.dot(inputs_bf.T, d_first, preferred_element_type=jnp.float32)
        firsts.append(grad_in)
        seconds.append(grad_mid)
        thirds.append(grad_out)
        adjoint = adjoint * factors[index]
    grad_z_part = jnp.sum(adjoint[:, None] * increments[0], axis=0)
    adjoint = adjoint * factors[0]
    grad_y_part = jnp.sum(adjoint)
    stack_first = jnp.stack(firsts[::-1])
    stack_second = jnp.stack(seconds[::-1])
    stack_third = jnp.stack(thirds[::-1])
    loss, grad_y, grad_z, stack_first, stack_second, stack_third = lax.psum(
        (loss_local, grad_y_part, grad_z_part, stack_first, stack_second, stack_third), "batch"
    )
    return (
        loss,
        grad_y,
        grad_z,
        stack_first.astype(jnp.bfloat16),
        stack_second.astype(jnp.bfloat16),
        stack_third.astype(jnp.bfloat16),
    )


def solution(mesh):
    placed = (
        P("dim"),
        P(),
        P("dim"),
        P(None, "batch", "dim"),
        P("batch"),
        P("dim"),
        P(None, None, "dim"),
        P(None, "dim", None),
        P(None, None, "dim"),
    )
    return jax.shard_map(
        local,
        mesh=mesh,
        in_specs=placed,
        out_specs=(
            P(),
            P(),
            P("dim"),
            P(None, None, "dim"),
            P(None, "dim", None),
            P(None, None, "dim"),
        ),
        check_vma=False,
    )
```

profile of v0, /device:TPU:0, one launch (start us, length us, event | category | flops | bytes accessed | tf_op | source)
XLA Modules:
  0.0 775.1 jit_solution(10410166071132102595)
XLA Ops:
  7.2 2.2 fusion.133
  10.5 8.6 %all_gather.36 = bf16[256,1024]{0,1:T(8,128)(2,1)S(1)} all-gather(bf16[256,256]{0,1:T(8,128)(2,1)S(1)} %get-tuple-element.35), channel_id=1, replica_groups=mesh['batch'=8,'dim'=4] {'dim'}, dimensions={1}, use_global_device_ids=true | all-gather | bytes 655360 | tf_op jit(solution)/shard_map/all_gather | solution.py:35
  25.4 1.7 fusion.129
  27.1 7.3 all_gather.40
  38.6 10.5 %all_gather.38 = bf16[256,1024]{0,1:T(8,128)(2,1)S(1)} all-gather(bf16[256,256]{0,1:T(8,128)(2,1)S(1)} %get-tuple-element.25), channel_id=1, replica_groups=mesh['batch'=8,'dim'=4] {'dim'}, dimensions={1}, use_global_device_ids=true | all-gather | bytes 655360 | tf_op jit(solution)/shard_map/all_gather | solution.py:35
  53.4 7.3 all_gather.42
  63.6 2.5 fusion.13
  67.9 10.0 %all_gather.37 = bf16[256,1024]{1,0:T(8,128)(2,1)S(1)} all-gather(bf16[256,256]{1,0:T(8,128)(2,1)S(1)} %tanh_convert_fusion.3), channel_id=1, replica_groups=mesh['batch'=8,'dim'=4] {'dim'}, dimensions={1}, use_global_device_ids=true | all-gather | bytes 655360 | tf_op jit(solution)/shard_map/all_gather | solution.py:44
  79.1 1.9 reduce-scatter.13.cloned.1.call-done
  82.0 6.9 all_gather.41
  90.1 19.3 %reduce-scatter.11.cloned.1.call-done = f32[256,256]{1,0:T(8,128)} async-done(((f32[256,1024]{1,0:T(8,128)}), f32[256,256]{1,0:T(8,128)}) %reduce-scatter.11.cloned.1.call-update) | async-done | bytes 262160 | tf_op jit(solution)/shard_map/reduce_scatter | solution.py:42
  110.4 6.6 all_gather.39
  118.1 19.0 %reduce-scatter.15.cloned.1.call-done = f32[256,256]{1,0:T(8,128)} async-done(((f32[256,1024]{1,0:T(8,128)}), f32[256,256]{1,0:T(8,128)}) %reduce-scatter.15.cloned.1.call-update) | async-done | bytes 262160 | tf_op jit(solution)/shard_map/reduce_scatter | solution.py:42
  138.1 6.6 all_gather.43
  145.9 6.8 all-reduce.1
  160.6 2.2 pad_maximum_fusion.2
  165.0 14.4 %reduce-scatter.23.cloned.1.call-done = f32[256,256]{1,0:T(8,128)} async-done(((f32[256,1024]{1,0:T(8,128)}), f32[256,256]{1,0:T(8,128)}) %reduce-scatter.23.cloned.1.call-update) | async-done | bytes 262160 | tf_op jit(solution)/shard_map/reduce_scatter | solution.py:63
  180.5 6.6 all_gather.47
  188.4 18.8 %reduce-scatter.21.cloned.1.call-done = f32[256,256]{1,0:T(8,128)} async-done(((f32[256,1024]{1,0:T(8,128)}), f32[256,256]{1,0:T(8,128)}) %reduce-scatter.21.cloned.1.call-update) | async-done | bytes 262160 | tf_op jit(solution)/shard_map/reduce_scatter | solution.py:63
  208.2 6.6 all_gather.46
  216.1 19.0 %reduce-scatter.19.cloned.1.call-done = f32[256,256]{1,0:T(8,128)} async-done(((f32[256,1024]{1,0:T(8,128)}), f32[256,256]{1,0:T(8,128)}) %reduce-scatter.19.cloned.1.call-update) | async-done | bytes 262160 | tf_op jit(solution)/shard_map/reduce_scatter | solution.py:63
  236.2 6.8 all_gather.45
  243.8 2.3 convolution_bitcast_fusion.6
  246.1 2.9 convolution_bitcast_fusion.8
  249.0 2.9 convolution_bitcast_fusion.9
  251.9 3.0 convolution_bitcast_fusion.10
  254.9 7.6 reduce-scatter.17.cloned.1.call-done
  263.6 6.6 all_gather.44
  270.2 1.9 convolution_bitcast_fusion.11
  273.3 4.4 pad_maximum_fusion
  277.7 2.3 pad_maximum_fusion.1
  279.9 488.3 %all-reduce.3 = (f32[]{:T(128)}, f32[]{:T(128)}, f32[256]{0:T(256)}, bf16[4,1024,256]{2,1,0:T(8,128)(2,1)}, bf16[4,256,1024]{2,1,0:T(8,128)(2,1)}, /*index=5*/bf16[4,1024,256]{2,1,0:T(8,128)(2,1)}) all-reduce(f32[]{:T(128)S(6)} %mul_shard_map.3, f32[]{:T(128)} %get-tuple-element.20, ...), channel_id=1, replica_groups=mesh['batch'=8,'dim'=4] {'batch'}, use_global_device_ids=true, to_apply=%region_17.0 | all-reduce | flops 3145986 | bytes 18876432 | tf_op jit(solution)/shard_map/psum | solution.py:80
  (129 shorter events, 45.5 us)
Async XLA Ops:
  7.2 2.5 copy-start.32
  7.2 2.5 copy-start.31
  7.2 59.7 %reduce-scatter.9.cloned.1.call-start = ((), (), s32[]{:S(2)}) async-start(), calls=%async_computation.8 | async-start | bytes 1310720 | tf_op jit(solution)/shard_map/reduce_scatter | solution.py:42
  9.4 11.4 %copy-start.1 = (bf16[4,256,1024]{2,1,0:T(8,128)(2,1)S(1)}, bf16[4,256,1024]{2,1,0:T(8,128)(2,1)}, u32[]{:S(2)}) copy-start(bf16[4,256,1024]{2,1,0:T(8,128)(2,1)} %param.16) | copy-start | bytes 6291460
  19.2 2.9 copy-start.23
  20.8 3.6 copy-start.16
  20.8 4.6 copy-start.33
  22.1 59.0 %reduce-scatter.13.cloned.1.call-start = ((), (), s32[]{:S(2)}) async-start(), calls=%async_computation.10 | async-start | bytes 1310720 | tf_op jit(solution)/shard_map/reduce_scatter | solution.py:42
  38.6 70.8 %reduce-scatter.11.cloned.1.call-start = ((), (), s32[]{:S(2)}) async-start(), calls=%async_computation.9 | async-start | bytes 1310720 | tf_op jit(solution)/shard_map/reduce_scatter | solution.py:42
  49.9 3.5 copy-start.30
  53.4 83.8 %reduce-scatter.15.cloned.1.call-start = ((), (), s32[]{:S(2)}) async-start(), calls=%async_computation.11 | async-start | bytes 1310720 | tf_op jit(solution)/shard_map/reduce_scatter | solution.py:42
  61.5 4.7 copy-start.34
  63.6 15.1 %copy-start = (bf16[4,1024,256]{2,1,0:T(8,128)(2,1)S(1)}, bf16[4,1024,256]{2,1,0:T(8,128)(2,1)}, u32[]{:S(2)}) copy-start(bf16[4,1024,256]{2,1,0:T(8,128)(2,1)} %param.17) | copy-start | bytes 6291460
  66.2 113.3 %reduce-scatter.23.cloned.1.call-start = ((), (), s32[]{:S(2)}) async-start(), calls=%async_computation.15 | async-start | bytes 1310720 | tf_op jit(solution)/shard_map/reduce_scatter | solution.py:63
  154.1 53.1 %reduce-scatter.21.cloned.1.call-start = ((), (), s32[]{:S(2)}) async-start(), calls=%async_computation.14 | async-start | bytes 1310720 | tf_op jit(solution)/shard_map/reduce_scatter | solution.py:63
  156.1 79.0 %reduce-scatter.19.cloned.1.call-start = ((), (), s32[]{:S(2)}) async-start(), calls=%async_computation.13 | async-start | bytes 1310720 | tf_op jit(solution)/shard_map/reduce_scatter | solution.py:63
  157.5 105.0 %reduce-scatter.17.cloned.1.call-start = ((), (), s32[]{:S(2)}) async-start(), calls=%async_computation.12 | async-start | bytes 1310720 | tf_op jit(solution)/shard_map/reduce_scatter | solution.py:63
  157.6 1.5 copy-start.6
  157.6 1.9 copy-start.9
  159.1 1.2 copy-start.4
  162.8 16.6 %copy-start.29 = (f32[256,256]{1,0:T(8,128)S(1)}, f32[256,256]{1,0:T(8,128)}, u32[]{:S(2)}) copy-start(f32[256,256]{1,0:T(8,128)} %reduce-scatter.15.cloned.1.call-done) | copy-start | bytes 786436
  163.6 23.4 %copy-start.22 = (f32[256,256]{1,0:T(8,128)S(1)}, f32[256,256]{1,0:T(8,128)}, u32[]{:S(2)}) copy-start(f32[256,256]{1,0:T(8,128)} %copy-done.21) | copy-start | bytes 786436
  165.0 42.3 %copy-start.28 = (f32[256,256]{1,0:T(8,128)S(1)}, f32[256,256]{1,0:T(8,128)}, u32[]{:S(2)}) copy-start(f32[256,256]{1,0:T(8,128)} %reduce-scatter.13.cloned.1.call-done) | copy-start | bytes 786436
  165.0 49.8 %copy-start.19 = (f32[256,256]{1,0:T(8,128)S(1)}, f32[256,256]{1,0:T(8,128)}, u32[]{:S(2)}) copy-start(f32[256,256]{1,0:T(8,128)} %copy-done.18) | copy-start | bytes 786436
  214.8 31.2 %copy-start.2 = (bf16[4,256,1024]{2,1,0:T(8,128)(2,1)S(1)}, bf16[4,256,1024]{2,1,0:T(8,128)(2,1)}, u32[]{:S(2)}) copy-start(bf16[4,256,1024]{2,1,0:T(8,128)(2,1)} %param.16) | copy-start | bytes 6291460
  249.0 2.9 copy-start.11
  251.9 18.3 %copy-start.17 = (f32[256,256]{1,0:T(8,128)S(1)}, f32[256,256]{1,0:T(8,128)}, u32[]{:S(2)}) copy-start(f32[256,256]{1,0:T(8,128)} %copy-done.16) | copy-start | bytes 786436
  251.9 18.3 %copy-start.24 = (bf16[256,1024]{0,1:T(8,128)(2,1)S(1)}, bf16[256,1024]{0,1:T(8,128)(2,1)}, u32[]{:S(2)}) copy-start(bf16[256,1024]{0,1:T(8,128)(2,1)} %copy-done.23) | copy-start | bytes 1572868
  272.1 1.2 copy-start.15
  273.3 4.4 copy-start.12
  273.3 4.4 copy-start.13
  273.3 4.4 copy-start.14
  (11 other events, 8.5 us)
Sparse Core Ops, SparseCore 0:
  22.2 28.4 reduce-scatter.8
  53.8 27.2 reduce-scatter.12
  84.2 25.1 reduce-scatter.10
  112.3 24.7 reduce-scatter.14
  154.2 25.1 reduce-scatter.22
  182.4 24.7 reduce-scatter.20
  210.3 24.7 reduce-scatter.18
  237.7 24.7 reduce-scatter.16
where the time goes:
time: 776 us; the launch traced here: 775 us
  blocking collectives  586 us (76%)
  waiting for transfers between devices  100 us (13%)
  matrix products  37.3 us (5%)
  other arithmetic  20.3 us (3%)
  between operations  15.9 us (2%)
  local copies, waits for them, and re-layouts  15.5 us (2%)
    psum x1, blocking collectives, local(): lax.psum((loss_local, grad_y_part, grad_z_part, stack_first, stack_second...  488 us
    reduce_scatter x4, waiting for transfers between devices, local(): lax.psum_scatter(back_part, 'dim', scatter_dimension=1, tiled=True)  59.8 us
    reduce_scatter x4, waiting for transfers between devices, local(): lax.psum_scatter(part_second, 'dim', scatter_dimension=1, tiled=True)  40.3 us
    all_gather x4, blocking collectives, local(): lax.all_gather(states.astype(jnp.bfloat16), 'dim', axis=1, tiled=True)  33.6 us
    all_gather x4, blocking collectives, local(): lax.all_gather(tanh_second.astype(jnp.bfloat16), 'dim', axis=1, tiled=True)  30.1 us
    all_gather x4, blocking collectives, local(): d_second = lax.all_gather(d_share, 'dim', axis=1, tiled=True)  26.6 us
  transfers between devices with their start and end apart: 8, of which 7 were waited for; matrix products, arithmetic and copies ran while one was open for 6% of the time, Pallas kernels for 0%

commit v1 on v0

--- a/solution.py
+++ b/solution.py
@@ -14,7 +14,7 @@
 DEFAULT_LOSS = 1.0 / 3.0
 
 
-def local(
+def local_dense(
     x_start, y_start, z_start, increments, default_step, term_weight, w_first, w_second, w_third
 ):
     steps = increments.shape[0]
@@ -90,6 +90,111 @@
     )
 
 
+def swap(value):
+    return lax.all_to_all(value, "dim", split_axis=0, concat_axis=0, tiled=True)
+
+
+def local_nets(
+    x_start, y_start, z_start, increments, default_step, term_weight, w_first, w_second, w_third
+):
+    f32, bf16 = jnp.float32, jnp.bfloat16
+    steps, paths, share = increments.shape
+    nets = steps - 1
+    width = w_first.shape[1]
+    hidden = w_second.shape[2]
+    rows = lax.axis_size("batch")
+    tstep = 1.0 / steps
+    scale = 1.0 / math.sqrt(paths * rows)
+    me = lax.axis_index("dim")
+    counter = jnp.arange(steps, dtype=jnp.int32)
+    factors = (
+        1.0
+        + DISCOUNT * tstep
+        - DEFAULT_LOSS * (counter[:, None] == default_step[None, :]).astype(f32)
+    )
+    states = jnp.broadcast_to(x_start[None, :], (paths, share))
+    dot_start = jnp.sum(increments[0] * z_start[None, :], axis=1)
+    sent = []
+    for index in range(steps):
+        if index > 0:
+            sent.append(states.astype(bf16))
+        states = states * (1.0 + DRIFT_RATE * tstep + VOLATILITY * increments[index])
+    target_part = jnp.sum(states * term_weight[None, :], axis=1) / math.sqrt(share * lax.axis_size("dim"))
+
+    def whole(value):
+        return jnp.transpose(swap(value), (1, 0, 2)).reshape(paths, width)
+
+    inputs = whole(jnp.stack(sent))
+    inc = whole(increments[1:])
+    third = swap(w_third)
+    first = swap(w_first)
+    second = swap(w_second).reshape(hidden, hidden)
+    first = jnp.transpose(first, (1, 0, 2)).reshape(width, hidden)
+    third = jnp.transpose(third, (1, 0, 2)).reshape(hidden, width)
+    high = inc.astype(bf16)
+    low = (inc - high.astype(f32)).astype(bf16)
+    back = jnp.dot(high, third.T, preferred_element_type=f32) + jnp.dot(
+        low, third.T, preferred_element_type=f32
+    )
+    tanh_first = jnp.tanh(jnp.dot(inputs, first, preferred_element_type=f32))
+    hidden_first = tanh_first.astype(bf16)
+    tanh_second = jnp.tanh(jnp.dot(hidden_first, second, preferred_element_type=f32))
+    hidden_second = tanh_second.astype(bf16)
+    dot_mine = jnp.sum(hidden_second.astype(f32) * back, axis=1)
+    slope_second = back * (1.0 - tanh_second * tanh_second)
+    slope_first = jnp.dot(slope_second.astype(bf16), second.T, preferred_element_type=f32) * (
+        1.0 - tanh_first * tanh_first
+    )
+    shared = lax.all_gather(jnp.stack([dot_mine, dot_start, target_part]), "dim")
+    value = factors[0] * y_start + jnp.sum(shared[:, 1], axis=0)
+    for index in range(1, steps):
+        value = factors[index] * value + shared[index - 1, 0]
+    error = value - jnp.sum(shared[:, 2], axis=0)
+    loss_local = scale * jnp.sum(error * error)
+    adjoint = 2.0 * scale * error
+    adjoints = []
+    for index in range(steps - 1, 0, -1):
+        adjoints.append(adjoint)
+        adjoint = adjoint * factors[index]
+    grad_z_part = jnp.sum(adjoint[:, None] * increments[0], axis=0)
+    grad_y_part = jnp.sum(adjoint * factors[0])
+    mine = lax.dynamic_index_in_dim(jnp.stack(adjoints[::-1]), me, keepdims=False)[:, None]
+    grad_third = jnp.dot(hidden_second.T, (mine * inc).astype(bf16), preferred_element_type=f32)
+    grad_second = jnp.dot(
+        hidden_first.T, (mine * slope_second).astype(bf16), preferred_element_type=f32
+    )
+    grad_first = jnp.dot(inputs.T, (mine * slope_first).astype(bf16), preferred_element_type=f32)
+
+    def columns(grad):
+        part = lax.psum_scatter(grad.astype(bf16), "batch", scatter_dimension=0, tiled=True)
+        part = jnp.transpose(part.reshape(part.shape[0], nets, -1), (1, 0, 2))
+        return lax.all_gather(swap(part), "batch", axis=1, tiled=True)
+
+    def lines(grad):
+        grad = grad.astype(bf16).reshape(nets, -1, grad.shape[1])
+        part = lax.psum_scatter(grad, "batch", scatter_dimension=1, tiled=True)
+        return lax.all_gather(swap(part), "batch", axis=1, tiled=True)
+
+    loss, grad_y, grad_z = lax.psum((loss_local, grad_y_part, grad_z_part), "batch")
+    return (
+        loss,
+        grad_y,
+        grad_z,
+        columns(grad_first),
+        lines(grad_second),
+        columns(grad_third),
+    )
+
+
+def pick(mesh):
+    def run(*args):
+        nets = args[6].shape[0]
+        fits = mesh.shape["dim"] == nets
+        return (local_nets if fits else local_dense)(*args)
+
+    return run
+
+
 def solution(mesh):
     placed = (
         P("dim"),
@@ -103,7 +208,7 @@
         P(None, None, "dim"),
     )
     return jax.shard_map(
-        local,
+        pick(mesh),
         mesh=mesh,
         in_specs=placed,
         out_specs=(

time: 776 us -> 523 us (0.67)
  blocking collectives: 586 us -> 101 us
  waiting for transfers between devices: 100 us -> 352 us
  matrix products: 37.3 us -> 16.5 us
  other arithmetic: 20.3 us -> 3.81 us
  starting transfers between devices: 0.33 us -> 11.9 us
    psum x2 -> x1, blocking collectives: 495 us -> 20.2 us  [local_nets(): lax.psum((loss_local, grad_y_part, grad_z_part), 'batch')]
    all_gather x0 -> x3, waiting for transfers between devices: none -> 118 us  [the longest x2 68 us: columns(): return lax.all_gather(swap(part), 'batch', axis=1, tiled=True)]
    reduce_scatter x8 -> x3, waiting for transfers between devices: 100 us -> 186 us  [the longest x2 124 us: columns(): lax.psum_scatter(grad.astype(bf16), 'batch', scatter_dimension=0, tiled=T...]
    all_gather x12 -> x1, blocking collectives: 90.4 us -> 5.2 us  [local_nets(): lax.all_gather(jnp.stack([dot_mine, dot_start, target_part]), 'dim')]
    all_to_all x0 -> x5, blocking collectives: none -> 75.9 us  [swap(): return lax.all_to_all(value, 'dim', split_axis=0, concat_axis=0, tiled=True)]
    all_to_all x0 -> x3, waiting for transfers between devices: none -> 48.5 us  [swap(): return lax.all_to_all(value, 'dim', split_axis=0, concat_axis=0, tiled=True)]
    dot_general x28 -> x7, matrix products: 37.3 us -> 16.5 us  [the longest x1 4.97 us: local_nets(): jnp.dot(inputs.T, (mine * slope_first).astype(bf16), preferred_element_ty...]
    all_to_all x0 -> x3, starting transfers between devices: none -> 11.6 us  [swap(): return lax.all_to_all(value, 'dim', split_axis=0, concat_axis=0, tiled=True)]
  transfers between devices with their start and end apart: 8 -> 9, of which waited for: 7 -> 9; matrix products, arithmetic and copies ran while one was open for 6% -> 3% of each run, Pallas kernels for 0% -> 0%
where the time goes in v1:
time: 523 us; the launch traced here: 522 us
  waiting for transfers between devices  352 us (67%)
  blocking collectives  101 us (19%)
  local copies, waits for them, and re-layouts  20.5 us (4%)
  matrix products  16.5 us (3%)
  between operations  15.7 us (3%)
  starting transfers between devices  11.9 us (2%)
    reduce_scatter x2, waiting for transfers between devices, columns(): lax.psum_scatter(grad.astype(bf16), 'batch', scatter_dimension=0, tiled=T...  124 us
    all_to_all x5, blocking collectives, swap(): return lax.all_to_all(value, 'dim', split_axis=0, concat_axis=0, tiled=True)  75.9 us
    all_gather x2, waiting for transfers between devices, columns(): return lax.all_gather(swap(part), 'batch', axis=1, tiled=True)  68 us
    reduce_scatter x1, waiting for transfers between devices, lines(): part = lax.psum_scatter(grad, 'batch', scatter_dimension=1, tiled=True)  61.9 us
    all_gather x1, waiting for transfers between devices, lines(): return lax.all_gather(swap(part), 'batch', axis=1, tiled=True)  49.7 us
    all_to_all x3, waiting for transfers between devices, swap(): return lax.all_to_all(value, 'dim', split_axis=0, concat_axis=0, tiled=True)  48.5 us
    psum x1, blocking collectives, local_nets(): lax.psum((loss_local, grad_y_part, grad_z_part), 'batch')  20.2 us
    unnamed x43, local copies, waits for them, and re-layouts  16.4 us
  transfers between devices with their start and end apart: 9, of which 9 were waited for; matrix products, arithmetic and copies ran while one was open for 3% of the time, Pallas kernels for 0%

profile of v1, /device:TPU:0, one launch (start us, length us, event | category | flops | bytes accessed | tf_op | source)
XLA Modules:
  0.0 521.5 jit_solution(17341776108765695001)
XLA Ops:
  7.2 2.1 fusion.53
  11.2 4.2 all-to-all-start
  15.5 8.8 %all-to-all-done = bf16[4,256,256]{1,2,0:T(8,128)(2,1)S(1)} async-done(((bf16[4,256,256]{1,2,0:T(8,128)(2,1)}), bf16[4,256,256]{1,2,0:T(8,128)(2,1)S(1)}, u32[]{:S(2)}, u32[]{:S(2)}) %all-to-all-start) | async-done | bytes 524320 | tf_op jit(solution)/shard_map/all_to_all | solution.py:94
  24.3 17.6 %all_to_all.40 = f32[4,256,256]{2,1,0:T(8,128)} all-to-all(f32[4,256,256]{2,1,0:T(8,128)S(1)} %slice-done), channel_id=1, replica_groups=mesh['batch'=8,'dim'=4] {'dim'}, dimensions={0} | all-to-all | bytes 2097152 | tf_op jit(solution)/shard_map/all_to_all | solution.py:94
  41.8 3.6 all-to-all-start.2
  45.5 4.0 copy.31
  49.4 21.7 %all-to-all-done.2 = bf16[4,256,1024]{2,1,0:T(8,128)(2,1)S(1)} async-done(((bf16[4,256,1024]{2,1,0:T(8,128)(2,1)}), bf16[4,256,1024]{2,1,0:T(8,128)(2,1)S(1)}, u32[]{:S(2)}, u32[]{:S(2)}) %all-to-all-start.2) | async-done | bytes 2097184 | tf_op jit(solution)/shard_map/all_to_all | solution.py:94
  71.1 30.1 %all_to_all.41 = bf16[4,1024,256]{1,2,0:T(8,128)(2,1)} all-to-all(bf16[4,1024,256]{1,2,0:T(8,128)(2,1)} %copy.31), channel_id=1, replica_groups=mesh['batch'=8,'dim'=4] {'dim'}, dimensions={0} | all-to-all | bytes 4194304 | tf_op jit(solution)/shard_map/all_to_all | solution.py:94
  101.2 3.8 all-to-all-start.4
  106.8 1.3 fusion.27
  108.2 2.7 convolution_tanh_fusion.1
  112.6 18.0 %all-to-all-done.4 = bf16[4,1024,256]{2,1,0:T(8,128)(2,1)S(1)} async-done(((bf16[4,1024,256]{2,1,0:T(8,128)(2,1)}), bf16[4,1024,256]{2,1,0:T(8,128)(2,1)S(1)}, u32[]{:S(2)}, u32[]{:S(2)}) %all-to-all-start.4) | async-done | bytes 2097184 | tf_op jit(solution)/shard_map/all_to_all | solution.py:94
  130.6 2.0 fusion.4
  132.7 1.8 multiply_reduce_fusion
  134.5 5.2 all-gather.1
  139.7 5.0 convolution_convert_fusion.2
  146.3 2.2 convolution_convert_fusion.1
  148.5 1.1 copy-done.5
  149.8 2.1 convolution_convert_fusion
  152.0 62.3 %reduce-scatter.4.cloned.1.call-done = bf16[128,1024]{1,0:T(8,128)(2,1)} async-done(((bf16[1024,1024]{1,0:T(8,128)(2,1)}), bf16[128,1024]{1,0:T(8,128)(2,1)}) %reduce-scatter.4.cloned.1.call-update) | async-done | bytes 262160 | tf_op jit(solution)/shard_map/reduce_scatter | solution.py:169
  215.3 9.1 %all_to_all.42 = bf16[4,128,256]{2,1,0:T(8,128)(2,1)} all-to-all(bf16[4,128,256]{2,1,0:T(8,128)(2,1)S(1)} %bitcast.154), channel_id=1, replica_groups=mesh['batch'=8,'dim'=4] {'dim'}, dimensions={0} | all-to-all | bytes 524288 | tf_op jit(solution)/shard_map/all_to_all | solution.py:94
  224.4 61.9 %reduce-scatter.6.cloned.1.call-done = bf16[4,32,1024]{2,1,0:T(8,128)(2,1)} async-done(((bf16[4,256,1024]{2,1,0:T(8,128)(2,1)}), bf16[4,32,1024]{2,1,0:T(8,128)(2,1)}) %reduce-scatter.6.cloned.1.call-update) | async-done | bytes 262160 | tf_op jit(solution)/shard_map/reduce_scatter | solution.py:175
  286.4 10.1 %all_to_all.43 = bf16[4,32,1024]{2,1,0:T(8,128)(2,1)} all-to-all(bf16[4,32,1024]{2,1,0:T(8,128)(2,1)} %reduce-scatter.6.cloned.1.call-done), channel_id=1, replica_groups=mesh['batch'=8,'dim'=4] {'dim'}, dimensions={0} | all-to-all | bytes 524288 | tf_op jit(solution)/shard_map/all_to_all | solution.py:94
  296.5 61.3 %reduce-scatter.8.cloned.1.call-done = bf16[128,1024]{1,0:T(8,128)(2,1)} async-done(((bf16[1024,1024]{1,0:T(8,128)(2,1)}), bf16[128,1024]{1,0:T(8,128)(2,1)}) %reduce-scatter.8.cloned.1.call-update) | async-done | bytes 262160 | tf_op jit(solution)/shard_map/reduce_scatter | solution.py:169
  358.8 9.1 %all_to_all.44 = bf16[4,128,256]{2,1,0:T(8,128)(2,1)} all-to-all(bf16[4,128,256]{2,1,0:T(8,128)(2,1)S(1)} %bitcast.155), channel_id=1, replica_groups=mesh['batch'=8,'dim'=4] {'dim'}, dimensions={0} | all-to-all | bytes 524288 | tf_op jit(solution)/shard_map/all_to_all | solution.py:94
  369.9 20.2 %all-reduce = (f32[]{:T(128)}, f32[]{:T(128)}, f32[256]{0:T(256)}) all-reduce(f32[]{:T(128)S(6)} %mul_shard_map.3, f32[]{:T(128)} %get-tuple-element.17, f32[256]{0:T(256)S(1)} %fusion.30), channel_id=1, replica_groups=mesh['batch'=8,'dim'=4] {'batch'}, use_global_device_ids=true, to_apply=%region_6.0 | all-reduce | flops 258 | bytes 2064 | tf_op jit(solution)/shard_map/psum | solution.py:178
  390.1 18.3 %all-gather.6.cloned.1.call-done = bf16[4,1024,256]{2,1,0:T(8,128)(2,1)} async-done(((bf16[4,128,256]{2,1,0:T(8,128)(2,1)}), bf16[4,1024,256]{2,1,0:T(8,128)(2,1)}) %all-gather.6.cloned.1.call-update) | async-done | bytes 2097168 | tf_op jit(solution)/shard_map/all_gather | solution.py:171
  408.4 49.7 %all-gather.8.cloned.1.call-done = bf16[4,256,1024]{2,1,0:T(8,128)(2,1)} async-done(((bf16[4,32,1024]{2,1,0:T(8,128)(2,1)}), bf16[4,256,1024]{2,1,0:T(8,128)(2,1)}) %all-gather.8.cloned.1.call-update) | async-done | bytes 2097168 | tf_op jit(solution)/shard_map/all_gather | solution.py:176
  458.1 49.7 %all-gather.10.cloned.1.call-done = bf16[4,1024,256]{2,1,0:T(8,128)(2,1)} async-done(((bf16[4,128,256]{2,1,0:T(8,128)(2,1)}), bf16[4,1024,256]{2,1,0:T(8,128)(2,1)}) %all-gather.10.cloned.1.call-update) | async-done | bytes 2097168 | tf_op jit(solution)/shard_map/all_gather | solution.py:171
  507.8 3.2 copy.52
  511.0 1.3 copy.53
  513.3 1.3 copy.54
  (69 shorter events, 11.1 us)
Async XLA Ops:
  7.2 2.6 copy-start.13
  9.5 1.7 copy-start.9
  9.7 0.7 copy-start.10
  9.8 1.4 copy-start.8
  10.3 13.9 %slice-start = ((f32[5,256,256]{2,1,0:T(8,128)}), f32[4,256,256]{2,1,0:T(8,128)S(1)}, s32[]{:S(2)}) async-start(f32[5,256,256]{2,1,0:T(8,128)} %param.12), calls=%async_computation.17 | async-start | bytes 2097152 | tf_op jit(solution)/shard_map/slice | solution.py:128
  11.2 13.1 %all-to-all-start = ((bf16[4,256,256]{1,2,0:T(8,128)(2,1)}), bf16[4,256,256]{1,2,0:T(8,128)(2,1)S(1)}, u32[]{:S(2)}, u32[]{:S(2)}) async-start(bf16[4,256,256]{1,2,0:T(8,128)(2,1)} %pad_maximum_fusion), calls=%async_computation | async-start | bytes 1048576 | tf_op jit(solution)/shard_map/all_to_all | solution.py:94
  24.3 17.6 %copy-start.7 = (bf16[4,256,256]{1,2,0:T(8,128)(2,1)}, bf16[4,256,256]{1,2,0:T(8,128)(2,1)S(1)}, u32[]{:S(2)}) copy-start(bf16[4,256,256]{1,2,0:T(8,128)(2,1)S(1)} %all-to-all-done) | copy-start | bytes 1572868
  41.8 29.3 %all-to-all-start.2 = ((bf16[4,256,1024]{2,1,0:T(8,128)(2,1)}), bf16[4,256,1024]{2,1,0:T(8,128)(2,1)S(1)}, u32[]{:S(2)}, u32[]{:S(2)}) async-start(bf16[4,256,1024]{2,1,0:T(8,128)(2,1)} %param.16), calls=%async_computation.2 | async-start | bytes 4194304 | tf_op jit(solution)/shard_map/all_to_all | solution.py:94
  71.1 30.1 %copy-start = (bf16[4,256,1024]{2,1,0:T(8,128)(2,1)}, bf16[4,256,1024]{2,1,0:T(8,128)(2,1)S(1)}, u32[]{:S(2)}) copy-start(bf16[4,256,1024]{2,1,0:T(8,128)(2,1)S(1)} %all-to-all-done.2) | copy-start | bytes 6291460
  101.2 5.6 %copy-start.15 = (f32[256]{0:T(256)S(1)}, f32[256]{0:T(256)}, u32[]{:S(2)}) copy-start(f32[256]{0:T(256)} %param.11) | copy-start | bytes 3076
  101.2 5.6 %copy-start.16 = (f32[256]{0:T(256)S(1)}, f32[256]{0:T(256)}, u32[]{:S(2)}) copy-start(f32[256]{0:T(256)} %param.14) | copy-start | bytes 3076
  101.2 6.9 %copy-start.14 = (s32[256]{0:T(256)S(1)}, s32[256]{0:T(256)}, u32[]{:S(2)}) copy-start(s32[256]{0:T(256)} %param.13) | copy-start | bytes 3076
  101.2 29.4 %all-to-all-start.4 = ((bf16[4,1024,256]{2,1,0:T(8,128)(2,1)}), bf16[4,1024,256]{2,1,0:T(8,128)(2,1)S(1)}, u32[]{:S(2)}, u32[]{:S(2)}) async-start(bf16[4,1024,256]{2,1,0:T(8,128)(2,1)} %param.17), calls=%async_computation.4 | async-start | bytes 4194304 | tf_op jit(solution)/shard_map/all_to_all | solution.py:94
  105.0 109.3 %reduce-scatter.4.cloned.1.call-start = ((), (), s32[]{:S(2)}) async-start(), calls=%async_computation.11 | async-start | bytes 2359296 | tf_op jit(solution)/shard_map/reduce_scatter | solution.py:169
  108.1 3.7 copy-start.1
  110.9 1.0 copy-start.2
  130.6 2.1 copy-start.4
  144.7 1.2 copy-start.3
  144.7 1.5 copy-start.6
  144.7 141.6 %reduce-scatter.6.cloned.1.call-start = ((), (), s32[]{:S(2)}) async-start(), calls=%async_computation.13 | async-start | bytes 2359296 | tf_op jit(solution)/shard_map/reduce_scatter | solution.py:175
  148.4 1.2 copy-start.5
  148.5 209.4 %reduce-scatter.8.cloned.1.call-start = ((), (), s32[]{:S(2)}) async-start(), calls=%async_computation.15 | async-start | bytes 2359296 | tf_op jit(solution)/shard_map/reduce_scatter | solution.py:169
  152.0 256.5 %all-gather.6.cloned.1.call-start = ((), (), s32[]{:S(2)}) async-start(), calls=%async_computation.12 | async-start | bytes 2359296 | tf_op jit(solution)/shard_map/all_gather | solution.py:171
  224.4 233.8 %all-gather.8.cloned.1.call-start = ((), (), s32[]{:S(2)}) async-start(), calls=%async_computation.14 | async-start | bytes 2359296 | tf_op jit(solution)/shard_map/all_gather | solution.py:176
  296.5 211.3 %all-gather.10.cloned.1.call-start = ((), (), s32[]{:S(2)}) async-start(), calls=%async_computation.16 | async-start | bytes 2359296 | tf_op jit(solution)/shard_map/all_gather | solution.py:171
  507.8 3.2 copy-start.11
  511.0 2.3 copy-start.12
Sparse Core Ops, SparseCore 0:
  144.9 69.3 reduce-scatter.3
  218.4 67.9 reduce-scatter.5
  290.5 67.3 reduce-scatter.7
  359.9 48.5 all-gather.5
  410.5 47.5 all-gather.7
  460.2 47.5 all-gather.9

commit v2 on v1

--- a/solution.py
+++ b/solution.py
@@ -1,8 +1,11 @@
+import functools
 import math
 
 import jax
 import jax.numpy as jnp
 from jax import lax
+from jax.experimental import pallas as pl
+from jax.experimental.pallas import tpu as pltpu
 from jax.sharding import PartitionSpec as P
 
 D = 1024
@@ -90,8 +93,284 @@
     )
 
 
-def swap(value):
-    return lax.all_to_all(value, "dim", split_axis=0, concat_axis=0, tiled=True)
+MESH = pl.DeviceIdType.MESH
+PAIR = 2
+
+
+def remote(src, dst, sems, slot, target):
+    return pltpu.make_async_remote_copy(
+        src_ref=src,
+        dst_ref=dst,
+        send_sem=sems[0].at[slot],
+        recv_sem=sems[1].at[slot],
+        device_id=target,
+        device_id_type=MESH,
+    )
+
+
+def greet(targets):
+    barrier = pltpu.get_barrier_semaphore()
+    for target in targets:
+        pl.semaphore_signal(barrier, inc=1, device_id=target, device_id_type=MESH)
+    pl.semaphore_wait(barrier, len(targets))
+
+
+def fetch_kernel(nets, inc, state, third, first, second, inc_out, state_out, third_out, first_out, second_out, send, recv, far_send, far_recv, own):
+    row, me = lax.axis_index("batch"), lax.axis_index("dim")
+    side = lax.rem(row, PAIR)
+    beside = {"batch": row + 1 - 2 * side}
+    core, chip = lax.rem(me, PAIR), me // PAIR
+    chips = nets // PAIR
+    partner = chip * PAIR + 1 - core
+    far = [
+        (lax.rem(chip + jump, chips) * PAIR + lax.rem(core + turn, PAIR), lax.rem(chip + chips - jump, chips) * PAIR + lax.rem(core + turn, PAIR))
+        for jump in range(1, chips)
+        for turn in range(PAIR)
+    ]
+    share = inc.shape[2]
+    greet([beside, {"dim": partner}] + [{"dim": ahead} for ahead, _ in far])
+
+    def columns(source):
+        return pl.ds(pl.multiple_of(source * share, share), share)
+
+    def place(out, source, half, lines):
+        if lines:
+            depth = second.shape[1]
+            if half is None:
+                return out.at[pl.ds(pl.multiple_of(source * depth, depth), depth), :]
+            cut = depth // PAIR
+            return out.at[pl.ds(pl.multiple_of(source * depth + half * cut, cut), cut), :]
+        if half is None:
+            return out.at[:, columns(source)]
+        cut = out.shape[0] // PAIR
+        return out.at[pl.ds(pl.multiple_of(half * cut, cut), cut), columns(source)]
+
+    def piece(value, target, half):
+        if half is None:
+            return value.at[target]
+        cut = value.shape[1] // PAIR
+        return value.at[target, pl.ds(pl.multiple_of(half * cut, cut), cut), :]
+
+    whole = [(inc, inc_out), (state, state_out)]
+    split = [(third, third_out, False), (first, first_out, False), (second, second_out, True)]
+    every = [(value, out, False) for value, out in whole] + split
+    waits, forwards = [], []
+    slot = 0
+    for value, out in whole:
+        for ahead, _ in far:
+            copy = remote(piece(value, ahead, None), place(out, me, None, False), (send, recv), slot, {"dim": ahead})
+            copy.start()
+            waits.append(copy)
+            slot += 1
+    for value, out, lines in split:
+        for ahead, behind in far:
+            copy = remote(piece(value, ahead, side), place(out, me, side, lines), (send, recv), slot, {"dim": ahead})
+            copy.start()
+            forwards.append((copy, out, behind, lines))
+            slot += 1
+    locals_ = []
+    for index, (value, out, lines) in enumerate(every):
+        copy = remote(piece(value, partner, None), place(out, me, None, lines), (send, recv), slot, {"dim": partner})
+        copy.start()
+        waits.append(copy)
+        slot += 1
+        copy = pltpu.make_async_copy(piece(value, me, None), place(out, me, None, lines), own.at[index])
+        copy.start()
+        locals_.append(copy)
+    for index, (copy, out, behind, lines) in enumerate(forwards):
+        copy.wait_recv()
+        spot = place(out, behind, side, lines)
+        onward = remote(spot, spot, (far_send, far_recv), index, beside)
+        onward.start()
+        waits.append(onward)
+    for copy, _, _, _ in forwards:
+        copy.wait_send()
+    for copy in waits:
+        copy.wait()
+    for copy in locals_:
+        copy.wait()
+
+
+def fetch(inc, state, third, first, second):
+    nets = third.shape[0]
+    paths, width, hidden = inc.shape[1], first.shape[1], second.shape[2]
+    away = nets - PAIR
+    copies = 5 * away + 5
+    any_spec = pl.BlockSpec(memory_space=pl.ANY)
+    return pl.pallas_call(
+        functools.partial(fetch_kernel, nets),
+        out_shape=(
+            jax.ShapeDtypeStruct((paths, width), inc.dtype),
+            jax.ShapeDtypeStruct((paths, width), state.dtype),
+            jax.ShapeDtypeStruct((hidden, width), third.dtype),
+            jax.ShapeDtypeStruct((width, hidden), first.dtype),
+            jax.ShapeDtypeStruct((hidden, hidden), second.dtype),
+        ),
+        in_specs=[pl.BlockSpec(memory_space=pltpu.VMEM)] * 5,
+        out_specs=(any_spec,) * 5,
+        scratch_shapes=[
+            pltpu.SemaphoreType.DMA((copies,)),
+            pltpu.SemaphoreType.DMA((copies,)),
+            pltpu.SemaphoreType.DMA((3 * away,)),
+            pltpu.SemaphoreType.DMA((3 * away,)),
+            pltpu.SemaphoreType.DMA((5,)),
+        ],
+        compiler_params=pltpu.CompilerParams(
+            collective_id=0, has_side_effects=True, vmem_limit_bytes=16 * 1024 * 1024
+        ),
+        name="fetch",
+    )(inc, state, third, first, second)
+
+
+def reduce_kernel(rows, nets, *refs):
+    grads, small, outs, small_out = refs[0:3], refs[3], refs[4:7], refs[7]
+    near, passed, landed, total = refs[8:11], refs[11:14], refs[14:17], refs[17:20]
+    gathered = refs[20]
+    near_sems, deep_sems, dim_sems, deep_out, near_out, small_sems = (
+        (refs[21 + 2 * index], refs[22 + 2 * index]) for index in range(6)
+    )
+    own = refs[33]
+    f32, bf16 = jnp.float32, jnp.bfloat16
+    row, me = lax.axis_index("batch"), lax.axis_index("dim")
+    side, level = lax.rem(row, PAIR), row // PAIR
+    levels = rows // PAIR
+    beside = {"batch": row + 1 - 2 * side}
+    mats = range(3)
+    cuts = [grad.shape[1] // rows for grad in grads]
+
+    def at_level(jump):
+        return lax.rem(level + jump + levels, levels)
+
+    def lines(mat, owner):
+        return pl.ds(pl.multiple_of(owner * cuts[mat], cuts[mat]), cuts[mat])
+
+    greet(
+        [{"batch": lax.rem(row + jump, rows)} for jump in range(1, rows)]
+        + [{"dim": lax.rem(me + jump, nets)} for jump in range(1, nets)]
+    )
+    order = list(range(1, levels)) + [0]
+    waits = []
+    near_copies = {}
+    for jump in order:
+        for mat in mats:
+            owner = at_level(jump) * PAIR + 1 - side
+            copy = remote(
+                grads[mat].at[:, lines(mat, owner), :], near[mat].at[jump], near_sems, jump * 3 + mat, beside
+            )
+            copy.start()
+            near_copies[jump, mat] = copy
+    small_copies = []
+    for jump in range(1, rows):
+        copy = remote(small, gathered.at[row], small_sems, jump - 1, {"batch": lax.rem(row + jump, rows)})
+        copy.start()
+        small_copies.append(copy)
+    gathered[row] = small[...]
+    deep_copies = {}
+    for jump in order[:-1]:
+        for mat in mats:
+            near_copies[jump, mat].wait_recv()
+            owner = at_level(jump) * PAIR + side
+            both = grads[mat][:, lines(mat, owner), :].astype(f32) + near[mat][jump].astype(f32)
+            passed[mat][jump - 1] = both.astype(bf16)
+            copy = remote(
+                passed[mat].at[jump - 1], landed[mat].at[jump - 1], deep_sems, (jump - 1) * 3 + mat,
+                {"batch": owner},
+            )
+            copy.start()
+            deep_copies[jump, mat] = copy
+    dim_copies = {}
+    for mat in mats:
+        near_copies[0, mat].wait_recv()
+        entire = grads[mat][:, lines(mat, row), :].astype(f32) + near[mat][0].astype(f32)
+        for jump in order[:-1]:
+            deep_copies[jump, mat].wait_recv()
+            entire = entire + landed[mat][jump - 1].astype(f32)
+        total[mat][...] = entire.astype(bf16)
+        spot = outs[mat].at[me, lines(mat, row), :]
+        for jump in range(1, nets):
+            peer = lax.rem(me + jump, nets)
+            copy = remote(total[mat].at[peer], spot, dim_sems, (jump - 1) * 3 + mat, {"dim": peer})
+            copy.start()
+            dim_copies[jump, mat] = copy
+        copy = pltpu.make_async_copy(total[mat].at[me], spot, own.at[mat])
+        copy.start()
+        dim_copies[0, mat] = copy
+    out_copies = {}
+    for mat in mats:
+        dim_copies[0, mat].wait()
+        for jump in range(1, nets):
+            dim_copies[jump, mat].wait_recv()
+        spot = outs[mat].at[:, lines(mat, row), :]
+        for jump in range(1, levels):
+            copy = remote(
+                spot, spot, deep_out, (jump - 1) * 3 + mat, {"batch": at_level(jump) * PAIR + side}
+            )
+            copy.start()
+            out_copies[jump, mat] = copy
+        copy = remote(spot, spot, near_out, mat, beside)
+        copy.start()
+        waits.append(copy)
+    for jump in range(1, levels):
+        for mat in mats:
+            out_copies[jump, mat].wait_recv()
+            spot = outs[mat].at[:, lines(mat, at_level(-jump) * PAIR + side), :]
+            copy = remote(spot, spot, near_out, jump * 3 + mat, beside)
+            copy.start()
+            waits.append(copy)
+    for copy in small_copies:
+        copy.wait()
+    summed = gathered[0]
+    for index in range(1, rows):
+        summed = summed + gathered[index]
+    small_out[...] = summed
+    for group in (near_copies, deep_copies, out_copies):
+        for copy in group.values():
+            copy.wait_send()
+    for (jump, _), copy in dim_copies.items():
+        if jump > 0:
+            copy.wait_send()
+    for copy in waits:
+        copy.wait()
+
+
+def reduce_grads(grads, small, rows):
+    nets = grads[0].shape[0]
+    levels = rows // PAIR
+    bf16 = jnp.bfloat16
+    any_spec = pl.BlockSpec(memory_space=pl.ANY)
+    vmem = pl.BlockSpec(memory_space=pltpu.VMEM)
+
+    def pieces(*count):
+        return [
+            pltpu.VMEM(count + (nets, grad.shape[1] // rows, grad.shape[2]), bf16) for grad in grads
+        ]
+
+    def dma(count):
+        return [pltpu.SemaphoreType.DMA((count,))] * 2
+
+    return pl.pallas_call(
+        functools.partial(reduce_kernel, rows, nets),
+        out_shape=tuple(jax.ShapeDtypeStruct(grad.shape, bf16) for grad in grads)
+        + (jax.ShapeDtypeStruct(small.shape, small.dtype),),
+        in_specs=[vmem] * 4,
+        out_specs=(any_spec,) * 3 + (vmem,),
+        scratch_shapes=pieces(levels)
+        + pieces(levels - 1)
+        + pieces(levels - 1)
+        + pieces()
+        + [pltpu.VMEM((rows,) + small.shape, small.dtype)]
+        + dma(3 * levels)
+        + dma(3 * (levels - 1))
+        + dma(3 * (nets - 1))
+        + dma(3 * (levels - 1))
+        + dma(3 * levels)
+        + dma(rows - 1)
+        + [pltpu.SemaphoreType.DMA((3,))],
+        compiler_params=pltpu.CompilerParams(
+            collective_id=1, has_side_effects=True, vmem_limit_bytes=32 * 1024 * 1024
+        ),
+        name="reduce_grads",
+    )(*grads, small)
 
 
 def local_nets(
@@ -121,16 +400,9 @@
         states = states * (1.0 + DRIFT_RATE * tstep + VOLATILITY * increments[index])
     target_part = jnp.sum(states * term_weight[None, :], axis=1) / math.sqrt(share * lax.axis_size("dim"))
 
-    def whole(value):
-        return jnp.transpose(swap(value), (1, 0, 2)).reshape(paths, width)
-
-    inputs = whole(jnp.stack(sent))
-    inc = whole(increments[1:])
-    third = swap(w_third)
-    first = swap(w_first)
-    second = swap(w_second).reshape(hidden, hidden)
-    first = jnp.transpose(first, (1, 0, 2)).reshape(width, hidden)
-    third = jnp.transpose(third, (1, 0, 2)).reshape(hidden, width)
+    inc, inputs, third, first, second = fetch(
+        increments[1:], jnp.stack(sent), w_third, w_first, w_second
+    )
     high = inc.astype(bf16)
     low = (inc - high.astype(f32)).astype(bf16)
     back = jnp.dot(high, third.T, preferred_element_type=f32) + jnp.dot(
@@ -159,37 +431,31 @@
     grad_z_part = jnp.sum(adjoint[:, None] * increments[0], axis=0)
     grad_y_part = jnp.sum(adjoint * factors[0])
     mine = lax.dynamic_index_in_dim(jnp.stack(adjoints[::-1]), me, keepdims=False)[:, None]
-    grad_third = jnp.dot(hidden_second.T, (mine * inc).astype(bf16), preferred_element_type=f32)
+
+    def columns(left, right):
+        left = left.T
+        blocks = jnp.split(right, nets, axis=1)
+        return jnp.stack(
+            [jnp.dot(left, block, preferred_element_type=f32).astype(bf16) for block in blocks]
+        )
+
+    grad_third = columns(hidden_second, (mine * inc).astype(bf16))
     grad_second = jnp.dot(
         hidden_first.T, (mine * slope_second).astype(bf16), preferred_element_type=f32
-    )
-    grad_first = jnp.dot(inputs.T, (mine * slope_first).astype(bf16), preferred_element_type=f32)
-
-    def columns(grad):
-        part = lax.psum_scatter(grad.astype(bf16), "batch", scatter_dimension=0, tiled=True)
-        part = jnp.transpose(part.reshape(part.shape[0], nets, -1), (1, 0, 2))
-        return lax.all_gather(swap(part), "batch", axis=1, tiled=True)
-
-    def lines(grad):
-        grad = grad.astype(bf16).reshape(nets, -1, grad.shape[1])
-        part = lax.psum_scatter(grad, "batch", scatter_dimension=1, tiled=True)
-        return lax.all_gather(swap(part), "batch", axis=1, tiled=True)
-
-    loss, grad_y, grad_z = lax.psum((loss_local, grad_y_part, grad_z_part), "batch")
-    return (
-        loss,
-        grad_y,
-        grad_z,
-        columns(grad_first),
-        lines(grad_second),
-        columns(grad_third),
-    )
+    ).astype(bf16)
+    grad_first = columns(inputs, (mine * slope_first).astype(bf16))
+    small = jnp.zeros((8, share), f32)
+    small = small.at[0].set(grad_z_part).at[1].set(loss_local).at[2].set(grad_y_part)
+    grad_first, grad_second, grad_third, small = reduce_grads(
+        (grad_first, grad_second.reshape(nets, -1, hidden), grad_third), small, rows
+    )
+    return small[1, 0], small[2, 0], small[0], grad_first, grad_second, grad_third
 
 
 def pick(mesh):
     def run(*args):
         nets = args[6].shape[0]
-        fits = mesh.shape["dim"] == nets
+        fits = mesh.shape["dim"] == nets and nets % PAIR == 0 and mesh.shape["batch"] % PAIR == 0
         return (local_nets if fits else local_dense)(*args)
 
     return run

time: 523 us -> 287 us (0.55)
  the two profiles are of different devices: /device:TPU:0 before, /device:TPU:16 now
where the time goes in v2:
time: 287 us; the launch traced here: 286 us
  Pallas kernels  247 us (86%)
  matrix products  14.9 us (5%)
  other arithmetic  8.66 us (3%)
  local copies, waits for them, and re-layouts  8.19 us (3%)
  blocking collectives  5.21 us (2%)
    pallas_call x1, Pallas kernels, reduce_grads(): pl.pallas_call(functools.partial(reduce_kernel, rows, nets), out_shape=tu...  185 us
    pallas_call x1, Pallas kernels, fetch(): pl.pallas_call(functools.partial(fetch_kernel, nets), out_shape=(jax.Shap...  62.1 us

profile of v2, /device:TPU:16, one launch (start us, length us, event | category | flops | bytes accessed | tf_op | source)
XLA Modules:
  0.0 286.4 jit_solution(10062026986249659309)
XLA Ops:
  1.3 1.7 fusion.14
  3.0 0.7 select_subtract_fusion
  3.7 1.1 fusion.46
  4.8 1.3 fusion.34
  6.1 1.4 slice.111.inc
  7.5 62.1 %fetch.1 = (f32[256,1024]{1,0:T(8,128)S(1)}, bf16[256,1024]{1,0:T(8,128)(2,1)S(1)}, bf16[1024,1024]{1,0:T(8,128)(2,1)S(1)}, bf16[1024,1024]{1,0:T(8,128)(2,1)S(1)}, bf16[1024,1024]{1,0:T(8,128)(2,1)S(1)}) custom-call(f32[4,256,256]{2,1,0:T(8,128)S(1)} %slice.111.inc, bf16[4,256,256]{2,1,0:T(8,128)(2,1)S(1)} %pad_maximum_fusion.2.state, ...), custom_call_target="tpu_custom_call" | custom-call | tf_op jit(solution)/shard_map/fetch/pallas_call | solution.py:200
  69.7 0.7 convolution_tanh_fusion.1
  70.4 0.7 convolution_tanh_fusion
  71.2 0.8 fusion.19
  72.0 1.8 multiply_reduce_fusion
  73.7 5.2 %all-gather.1 = f32[4,3,256]{2,1,0:T(4,128)S(1)} all-gather(f32[1,3,256]{2,1,0:T(4,128)S(1)} %maximum_bitcast_fusion), channel_id=2, replica_groups=mesh['batch'=8,'dim'=4] {'dim'}, dimensions={0}, use_global_device_ids=true | all-gather | bytes 15360 | tf_op jit(solution)/shard_map/all_gather | solution.py:420
  79.0 0.6 multiply_reduce_fusion.1
  79.6 0.6 multiply_reduce_fusion.2
  80.9 1.1 fusion.17
  82.0 3.9 %fusion.1 = bf16[256,1024]{1,0:T(8,128)(2,1)} fusion(bf16[1024,1024]{1,0:T(8,128)(2,1)} %copy-done, f32[256,1024]{1,0:T(8,128)S(1)} %convolution_tanh_fusion.1, f32[256]{0:T(256)S(1)} %bitcast.113, f32[256,1024]{1,0:T(8,128)} %get-tuple-element.89, f32[256,1024]{1,0:T(8,128)} %copy-done.5), kind=kOutput, calls=%fused_computation.8 | convolution fusion | flops 539230208 | bytes 5768192 | tf_op jit(solution)/shard_map/dot_general | solution.py:417
  86.0 2.2 convolution_convert_fusion
  88.2 0.9 multiply_convert_fusion
  89.1 0.6 broadcast.154
  89.9 1.3 fusion.9
  91.2 1.3 fusion.8
  92.5 0.4 fusion.7
  92.9 0.4 fusion.6
  93.6 0.4 fusion.4
  94.3 0.4 fusion.2
  94.7 0.6 pad_maximum_fusion
  95.3 1.0 copy-done.1
  96.3 185.0 %reduce_grads.1 = (bf16[4,1024,256]{2,1,0:T(8,128)(2,1)S(1)}, bf16[4,256,1024]{2,1,0:T(8,128)(2,1)S(1)}, bf16[4,1024,256]{2,1,0:T(8,128)(2,1)S(1)}, f32[8,256]{1,0:T(8,128)S(1)}) custom-call(bf16[4,1024,256]{2,1,0:T(8,128)(2,1)S(1)} %get-tuple-element.90.refs_0_, bf16[4,256,1024]{2,1,0:T(8,128)(2,1)S(1)} %bitcast.112, ...), custom_call_target="tpu_custom_call" | custom-call | tf_op jit(solution)/shard_map/reduce_grads/pallas_call | solution.py:351
  281.3 0.6 slice.130
  281.9 0.5 fusion.49
  282.4 1.3 copy.21
  283.7 1.3 copy.22
  285.1 1.3 copy.23
  (32 shorter events, 1.0 us)
Async XLA Ops:
  1.3 6.2 %copy-start.4 = (bf16[4,256,1024]{2,1,0:T(8,128)(2,1)S(1)}, bf16[4,256,1024]{2,1,0:T(8,128)(2,1)}, u32[]{:S(2)}) copy-start(bf16[4,256,1024]{2,1,0:T(8,128)(2,1)} %second.1) | copy-start | bytes 6291460
  4.8 2.7 copy-start.2
  4.8 2.7 copy-start.3
  69.7 1.5 copy-start
  71.2 2.6 copy-start.5
  82.0 4.0 %copy-start.6 = (f32[256,1024]{1,0:T(8,128)S(1)}, f32[256,1024]{1,0:T(8,128)}, u32[]{:S(2)}) copy-start(f32[256,1024]{1,0:T(8,128)} %copy-done.5) | copy-start | bytes 3145732
  82.0 4.0 %copy-start.7 = (f32[256,1024]{1,0:T(8,128)S(1)}, f32[256,1024]{1,0:T(8,128)}, u32[]{:S(2)}) copy-start(f32[256,1024]{1,0:T(8,128)} %get-tuple-element.89) | copy-start | bytes 3145732
  89.8 2.6 copy-start.9
  89.9 3.4 %copy-start.8 = (bf16[256,1024]{1,0:T(8,128)(2,1)S(1)}, bf16[256,1024]{1,0:T(8,128)(2,1)}, u32[]{:S(2)}) copy-start(bf16[256,1024]{1,0:T(8,128)(2,1)} %fusion.1) | copy-start | bytes 1572868
  94.7 1.6 copy-start.1

commit v3 on v1

--- a/solution.py
+++ b/solution.py
@@ -1,8 +1,11 @@
+import functools
 import math
 
 import jax
 import jax.numpy as jnp
 from jax import lax
+from jax.experimental import pallas as pl
+from jax.experimental.pallas import tpu as pltpu
 from jax.sharding import PartitionSpec as P
 
 D = 1024
@@ -90,8 +93,415 @@
     )
 
 
-def swap(value):
-    return lax.all_to_all(value, "dim", split_axis=0, concat_axis=0, tiled=True)
+MESH = pl.DeviceIdType.MESH
+PAIR = 2
+
+
+def remote(src, dst, sems, slot, target):
+    return pltpu.make_async_remote_copy(
+        src_ref=src,
+        dst_ref=dst,
+        send_sem=sems[0].at[slot],
+        recv_sem=sems[1].at[slot],
+        device_id=target,
+        device_id_type=MESH,
+    )
+
+
+def greet(targets):
+    barrier = pltpu.get_barrier_semaphore()
+    for target in targets:
+        pl.semaphore_signal(barrier, inc=1, device_id=target, device_id_type=MESH)
+    pl.semaphore_wait(barrier, len(targets))
+
+
+def flip(bit, turn):
+    return 1 - bit if turn else bit
+
+
+def here():
+    row, me = lax.axis_index("batch"), lax.axis_index("dim")
+    return row // PAIR, lax.rem(row, PAIR), me // PAIR, lax.rem(me, PAIR)
+
+
+def device(level, side, chip, core):
+    return {"batch": level * PAIR + side, "dim": chip * PAIR + core}
+
+
+def hop(level, bit):
+    low, high = lax.rem(level, PAIR), level // PAIR
+    return flip(high, bit == 1) * PAIR + flip(low, bit == 0)
+
+
+FLIPS = [(up, across, turn) for up in range(2) for across in range(2) for turn in range(2)]
+
+
+def fetch_kernel(inc, state, third, first, second, inc_out, state_out, third_out, first_out, second_out, *sems):
+    path_sems, core_sems, chip_sems, level_sems, pass_sems, last_sems = (
+        (sems[2 * index], sems[2 * index + 1]) for index in range(6)
+    )
+    own, own_path = sems[12], sems[13]
+    level, side, chip, core = here()
+    me = chip * PAIR + core
+    net = chip * PAIR + side
+    across = (1 - chip) * PAIR + core
+    partner = device(level, side, chip, 1 - core)
+    beyond = device(level, side, 1 - chip, core)
+    above = device(hop(level, 0), side, chip, core)
+    half = lax.rem(level, PAIR)
+    share, depth = inc.shape[2], second.shape[1]
+    greet(
+        [device(level, flip(side, up), flip(chip, ac), flip(core, turn)) for up, ac, turn in FLIPS[1:]]
+        + [above]
+    )
+
+    def columns(source):
+        return pl.ds(pl.multiple_of(source * share, share), share)
+
+    def place(out, source, lines, part):
+        if lines:
+            cut = depth if part is None else depth // PAIR
+            start = source * depth if part is None else source * depth + part * cut
+            return out.at[pl.ds(pl.multiple_of(start, cut), cut), :]
+        if part is None:
+            return out.at[:, columns(source)]
+        cut = out.shape[0] // PAIR
+        return out.at[pl.ds(pl.multiple_of(part * cut, cut), cut), columns(source)]
+
+    mats = [(third, third_out, False), (first, first_out, False), (second, second_out, True)]
+    paths = [(inc, inc_out), (state, state_out)]
+
+    def path_copy(index, up, ac):
+        value, out = paths[index]
+        to_chip, to_side = flip(chip, ac), flip(side, up)
+        slot = ((index * 2 + up) * 2 + ac) * PAIR + core
+        return remote(
+            value.at[to_chip * PAIR + to_side], out.at[:, columns(me)], path_sems, slot,
+            device(level, to_side, to_chip, side),
+        )
+
+    def path_arrival(index, up, ac, source):
+        value, out = paths[index]
+        slot = ((index * 2 + up) * 2 + ac) * PAIR + source
+        return remote(value.at[0], out.at[:, columns(me)], path_sems, slot, partner)
+
+    def path_own(index):
+        value, out = paths[index]
+        return pltpu.make_async_copy(value.at[net], out.at[:, columns(me)], own_path.at[index])
+
+    aligned = core == side
+    for index in range(2):
+        for up, ac in ((0, 1), (1, 1), (1, 0)):
+            path_copy(index, up, ac).start()
+    chip_copies, waits = [], []
+    for index, (value, out, lines) in enumerate(mats):
+        cut = value.shape[1] // PAIR
+        copy = remote(
+            value.at[(1 - chip) * PAIR + side, pl.ds(pl.multiple_of(half * cut, cut), cut), :],
+            place(out, me, lines, half), chip_sems, index, beyond,
+        )
+        copy.start()
+        chip_copies.append(copy)
+
+    @pl.when(aligned)
+    def _():
+        for index in range(2):
+            path_own(index).start()
+
+    @pl.when(jnp.logical_not(aligned))
+    def _():
+        for index in range(2):
+            path_copy(index, 0, 0).start()
+
+    for index, (value, out, lines) in enumerate(mats):
+        copy = remote(value.at[net], place(out, me, lines, None), core_sems, index, partner)
+        copy.start()
+        waits.append(copy)
+        copy = pltpu.make_async_copy(value.at[net], place(out, me, lines, None), own.at[index])
+        copy.start()
+        waits.append(copy)
+    level_copies = []
+    for index, (value, out, lines) in enumerate(mats):
+        chip_copies[index].wait_recv()
+        spot = place(out, across, lines, half)
+        copy = remote(spot, spot, level_sems, index, above)
+        copy.start()
+        level_copies.append(copy)
+        copy = remote(spot, spot, pass_sems, index, partner)
+        copy.start()
+        waits.append(copy)
+    for index, (value, out, lines) in enumerate(mats):
+        level_copies[index].wait_recv()
+        spot = place(out, across, lines, 1 - half)
+        copy = remote(spot, spot, last_sems, index, partner)
+        copy.start()
+        waits.append(copy)
+    for copy in chip_copies + level_copies:
+        copy.wait_send()
+    for index in range(2):
+        for up, ac in ((0, 1), (1, 1), (1, 0)):
+            path_copy(index, up, ac).wait_send()
+
+    @pl.when(aligned)
+    def _():
+        for index in range(2):
+            path_own(index).wait()
+            path_arrival(index, 0, 0, 1 - core).wait_recv()
+            for source in range(PAIR):
+                path_arrival(index, 0, 1, source).wait_recv()
+
+    @pl.when(jnp.logical_not(aligned))
+    def _():
+        for index in range(2):
+            path_copy(index, 0, 0).wait_send()
+            for ac in range(2):
+                for source in range(PAIR):
+                    path_arrival(index, 1, ac, source).wait_recv()
+
+    for copy in waits:
+        copy.wait()
+
+
+def fetch(inc, state, third, first, second):
+    nets = third.shape[0]
+    paths, width, hidden = inc.shape[1], first.shape[1], second.shape[2]
+    any_spec = pl.BlockSpec(memory_space=pl.ANY)
+    counts = [4 * nets, 3, 3, 3, 3, 3]
+    return pl.pallas_call(
+        fetch_kernel,
+        out_shape=(
+            jax.ShapeDtypeStruct((paths, width), inc.dtype),
+            jax.ShapeDtypeStruct((paths, width), state.dtype),
+            jax.ShapeDtypeStruct((hidden, width), third.dtype),
+            jax.ShapeDtypeStruct((width, hidden), first.dtype),
+            jax.ShapeDtypeStruct((hidden, hidden), second.dtype),
+        ),
+        in_specs=[pl.BlockSpec(memory_space=pltpu.VMEM)] * 5,
+        out_specs=(any_spec,) * 5,
+        scratch_shapes=[pltpu.SemaphoreType.DMA((count,)) for count in counts for _ in range(2)]
+        + [pltpu.SemaphoreType.DMA((3,)), pltpu.SemaphoreType.DMA((2,))],
+        compiler_params=pltpu.CompilerParams(
+            collective_id=0, has_side_effects=True, vmem_limit_bytes=16 * 1024 * 1024
+        ),
+        name="fetch",
+    )(inc, state, third, first, second)
+
+
+def share_kernel(block, out, gathered, send, recv):
+    level, side, chip, core = here()
+    targets = [device(level, flip(side, up), flip(chip, ac), flip(core, turn)) for up, ac, turn in FLIPS[1:]]
+    greet(targets)
+    copies = []
+    for index, target in enumerate(targets):
+        copy = remote(block, gathered.at[side, chip * PAIR + core], (send, recv), index, target)
+        copy.start()
+        copies.append(copy)
+    gathered[side, chip * PAIR + core] = block[...]
+    for copy in copies:
+        copy.wait()
+    out[...] = gathered[...]
+
+
+def share_level(block, nets):
+    shape = (PAIR, nets) + block.shape
+    vmem = pl.BlockSpec(memory_space=pltpu.VMEM)
+    return pl.pallas_call(
+        share_kernel,
+        out_shape=jax.ShapeDtypeStruct(shape, block.dtype),
+        in_specs=[vmem],
+        out_specs=vmem,
+        scratch_shapes=[pltpu.VMEM(shape, block.dtype)]
+        + [pltpu.SemaphoreType.DMA((len(FLIPS) - 1,))] * 2,
+        compiler_params=pltpu.CompilerParams(collective_id=2, has_side_effects=True),
+        name="share_level",
+    )(block)
+
+
+def reduce_kernel(rows, nets, *refs):
+    grads, small, outs, small_out = refs[0:3], refs[3], refs[4:7], refs[7]
+    zero, one, two = refs[8:11], refs[11:14], refs[14:17]
+    sent_one, sent_two, held = refs[17:20], refs[20:23], refs[23:26]
+    gathered = refs[26]
+    zero_sems, one_sems, two_sems, back_two, back_one, out_sems, small_sems = (
+        (refs[27 + 2 * index], refs[28 + 2 * index]) for index in range(7)
+    )
+    own = refs[41]
+    f32, bf16 = jnp.float32, jnp.bfloat16
+    level, side, chip, core = here()
+    row = level * PAIR + side
+    net = chip * PAIR + side
+    low, high = lax.rem(level, PAIR), level // PAIR
+    slot_mine = low * PAIR + high
+    partner = device(level, side, chip, 1 - core)
+    first, second = (device(hop(level, bit), side, chip, core) for bit in range(2))
+    mats = range(3)
+    cuts = [grad.shape[1] // rows for grad in grads]
+    chunks = [(mat, turn) for turn in (1, 0) for mat in (2, 1, 0)]
+    others = [(up, ac, turn) for up, ac, turn in FLIPS if (up, ac, turn) != (0, 0, 0)]
+    greet(
+        [{"batch": lax.rem(row + jump, rows)} for jump in range(1, rows)]
+        + [device(level, flip(side, up), flip(chip, ac), flip(core, turn)) for up, ac, turn in others if ac or turn]
+    )
+
+    def shards(turn):
+        return pl.ds(flip(chip, turn) * PAIR, PAIR)
+
+    def span(mat, start, count):
+        return pl.ds(pl.multiple_of(start * cuts[mat], cuts[mat]), count * cuts[mat])
+
+    copies = {}
+
+    def core_step(index):
+        mat, turn = chunks[index]
+        copy = remote(
+            grads[mat].at[shards(turn), span(mat, (1 - core) * 4, 4), :],
+            zero[mat].at[shards(turn)], zero_sems, index, partner,
+        )
+        copy.start()
+        copies["zero", index] = copy
+
+    def low_step(index):
+        mat, turn = chunks[index]
+        copies["zero", index].wait_recv()
+        start = (1 - low) * 2
+        value = grads[mat][shards(turn), span(mat, core * 4 + start, 2), :].astype(f32)
+        value = value + zero[mat][shards(turn), span(mat, start, 2), :].astype(f32)
+        sent_one[mat][shards(turn)] = value.astype(bf16)
+        copy = remote(
+            sent_one[mat].at[shards(turn)], one[mat].at[shards(turn)], one_sems, index, first
+        )
+        copy.start()
+        copies["one", index] = copy
+
+    def partial(mat, turn, end):
+        value = grads[mat][shards(turn), span(mat, core * 4 + low * 2 + end, 1), :].astype(f32)
+        value = value + zero[mat][shards(turn), span(mat, low * 2 + end, 1), :].astype(f32)
+        return value + one[mat][shards(turn), span(mat, end, 1), :].astype(f32)
+
+    def high_step(index):
+        mat, turn = chunks[index]
+        copies["one", index].wait_recv()
+        sent_two[mat][shards(turn)] = partial(mat, turn, 1 - high).astype(bf16)
+        copy = remote(
+            sent_two[mat].at[shards(turn)], two[mat].at[shards(turn)], two_sems, index, second
+        )
+        copy.start()
+        copies["two", index] = copy
+
+    def spread(index, event, slot, count):
+        mat, turn = chunks[index]
+        lines = span(mat, core * 4 + slot, count)
+        for up in range(2):
+            for swapped in range(2):
+                shard = flip(chip, turn) * PAIR + flip(core, swapped)
+                src = held[mat].at[shard, span(mat, slot, count), :]
+                dst = outs[mat].at[net, lines, :]
+                if up or turn or swapped:
+                    number = ((index * 3 + event) * 2 + up) * 2 + swapped
+                    copy = remote(
+                        src, dst, out_sems, number,
+                        device(level, flip(side, up), flip(chip, turn), flip(core, swapped)),
+                    )
+                else:
+                    copy = pltpu.make_async_copy(src, dst, own.at[index * 3 + event])
+                copy.start()
+                copies["out", index, event, up, swapped] = copy
+
+    def final_step(index):
+        mat, turn = chunks[index]
+        copies["two", index].wait_recv()
+        value = partial(mat, turn, high) + two[mat][shards(turn)].astype(f32)
+        held[mat][shards(turn), span(mat, slot_mine, 1), :] = value.astype(bf16)
+        spot = held[mat].at[shards(turn), span(mat, slot_mine, 1), :]
+        for name, sems, target in (("back_two", back_two, second), ("back_one", back_one, first)):
+            copy = remote(spot, spot, sems, index * 2 if name == "back_one" else index, target)
+            copy.start()
+            copies[name, index] = copy
+        spread(index, 0, slot_mine, 1)
+
+    def gather_step(index):
+        mat, turn = chunks[index]
+        copies["back_two", index].wait_recv()
+        slot = low * PAIR + 1 - high
+        spot = held[mat].at[shards(turn), span(mat, slot, 1), :]
+        copy = remote(spot, spot, back_one, index * 2 + 1, first)
+        copy.start()
+        copies["back_far", index] = copy
+        spread(index, 1, slot, 1)
+
+    def last_step(index):
+        copies["back_one", index].wait_recv()
+        copies["back_far", index].wait_recv()
+        spread(index, 2, (1 - low) * PAIR, PAIR)
+
+    for index in range(len(chunks)):
+        core_step(index)
+    small_copies = []
+    for jump in range(1, rows):
+        copy = remote(small, gathered.at[row], small_sems, jump - 1, {"batch": lax.rem(row + jump, rows)})
+        copy.start()
+        small_copies.append(copy)
+    gathered[row] = small[...]
+    stages = (low_step, high_step, final_step, gather_step, last_step)
+    for time in range(len(chunks) + len(stages) - 1):
+        for lag in reversed(range(len(stages))):
+            if 0 <= time - lag < len(chunks):
+                stages[lag](time - lag)
+    for copy in small_copies:
+        copy.wait()
+    summed = gathered[0]
+    for index in range(1, rows):
+        summed = summed + gathered[index]
+    small_out[...] = summed
+    for name, copy in copies.items():
+        if name[0] == "out":
+            copy.wait()
+        else:
+            copy.wait_send()
+
+
+def reduce_grads(grads, small, rows):
+    nets = grads[0].shape[0]
+    bf16 = jnp.bfloat16
+    any_spec = pl.BlockSpec(memory_space=pl.ANY)
+    vmem = pl.BlockSpec(memory_space=pltpu.VMEM)
+    chunks = 3 * PAIR
+
+    def pieces(count):
+        return [
+            pltpu.VMEM((nets, count * (grad.shape[1] // rows), grad.shape[2]), bf16)
+            for grad in grads
+        ]
+
+    def dma(count):
+        return [pltpu.SemaphoreType.DMA((count,))] * 2
+
+    return pl.pallas_call(
+        functools.partial(reduce_kernel, rows, nets),
+        out_shape=tuple(jax.ShapeDtypeStruct(grad.shape, bf16) for grad in grads)
+        + (jax.ShapeDtypeStruct(small.shape, small.dtype),),
+        in_specs=[vmem] * 4,
+        out_specs=(any_spec,) * 3 + (vmem,),
+        scratch_shapes=pieces(4)
+        + pieces(2)
+        + pieces(1)
+        + pieces(2)
+        + pieces(1)
+        + pieces(4)
+        + [pltpu.VMEM((rows,) + small.shape, small.dtype)]
+        + dma(chunks)
+        + dma(chunks)
+        + dma(chunks)
+        + dma(chunks)
+        + dma(chunks * 2)
+        + dma(chunks * 12)
+        + dma(rows - 1)
+        + [pltpu.SemaphoreType.DMA((chunks * 3,))],
+        compiler_params=pltpu.CompilerParams(
+            collective_id=1, has_side_effects=True, vmem_limit_bytes=36 * 1024 * 1024
+        ),
+        name="reduce_grads",
+    )(*grads, small)
 
 
 def local_nets(
@@ -107,11 +517,6 @@
     scale = 1.0 / math.sqrt(paths * rows)
     me = lax.axis_index("dim")
     counter = jnp.arange(steps, dtype=jnp.int32)
-    factors = (
-        1.0
-        + DISCOUNT * tstep
-        - DEFAULT_LOSS * (counter[:, None] == default_step[None, :]).astype(f32)
-    )
     states = jnp.broadcast_to(x_start[None, :], (paths, share))
     dot_start = jnp.sum(increments[0] * z_start[None, :], axis=1)
     sent = []
@@ -121,16 +526,9 @@
         states = states * (1.0 + DRIFT_RATE * tstep + VOLATILITY * increments[index])
     target_part = jnp.sum(states * term_weight[None, :], axis=1) / math.sqrt(share * lax.axis_size("dim"))
 
-    def whole(value):
-        return jnp.transpose(swap(value), (1, 0, 2)).reshape(paths, width)
-
-    inputs = whole(jnp.stack(sent))
-    inc = whole(increments[1:])
-    third = swap(w_third)
-    first = swap(w_first)
-    second = swap(w_second).reshape(hidden, hidden)
-    first = jnp.transpose(first, (1, 0, 2)).reshape(width, hidden)
-    third = jnp.transpose(third, (1, 0, 2)).reshape(hidden, width)
+    inc, inputs, third, first, second = fetch(
+        increments[1:], jnp.stack(sent), w_third, w_first, w_second
+    )
     high = inc.astype(bf16)
     low = (inc - high.astype(f32)).astype(bf16)
     back = jnp.dot(high, third.T, preferred_element_type=f32) + jnp.dot(
@@ -145,51 +543,62 @@
     slope_first = jnp.dot(slope_second.astype(bf16), second.T, preferred_element_type=f32) * (
         1.0 - tanh_first * tanh_first
     )
-    shared = lax.all_gather(jnp.stack([dot_mine, dot_start, target_part]), "dim")
-    value = factors[0] * y_start + jnp.sum(shared[:, 1], axis=0)
+    block = jnp.zeros((8, paths), f32)
+    block = block.at[0].set(dot_mine).at[1].set(dot_start).at[2].set(target_part)
+    block = block.at[3].set(default_step.astype(f32))
+    shared = share_level(block, nets)
+    side, core = lax.rem(lax.axis_index("batch"), PAIR), lax.rem(me, PAIR)
+    net = me // PAIR * PAIR + side
+    falls = shared[:, 0, 3]
+    factors = (
+        1.0
+        + DISCOUNT * tstep
+        - DEFAULT_LOSS * (counter[:, None, None].astype(f32) == falls[None]).astype(f32)
+    )
+    value = factors[0] * y_start + jnp.sum(shared[:, :, 1], axis=1)
     for index in range(1, steps):
-        value = factors[index] * value + shared[index - 1, 0]
-    error = value - jnp.sum(shared[:, 2], axis=0)
-    loss_local = scale * jnp.sum(error * error)
+        chip, low = divmod(index - 1, PAIR)
+        dots = shared[low, chip * PAIR : (chip + 1) * PAIR, 0]
+        value = factors[index] * value + dots
+    error = value - jnp.sum(shared[:, :, 2], axis=1)
     adjoint = 2.0 * scale * error
     adjoints = []
     for index in range(steps - 1, 0, -1):
         adjoints.append(adjoint)
         adjoint = adjoint * factors[index]
-    grad_z_part = jnp.sum(adjoint[:, None] * increments[0], axis=0)
-    grad_y_part = jnp.sum(adjoint * factors[0])
-    mine = lax.dynamic_index_in_dim(jnp.stack(adjoints[::-1]), me, keepdims=False)[:, None]
-    grad_third = jnp.dot(hidden_second.T, (mine * inc).astype(bf16), preferred_element_type=f32)
+    start = lax.dynamic_index_in_dim(adjoint, side, keepdims=False)
+    grad_z_part = jnp.sum(start[:, None] * increments[0], axis=0)
+    grad_y_part = jnp.sum(start * lax.dynamic_index_in_dim(factors[0], side, keepdims=False))
+    fault = lax.dynamic_index_in_dim(error, side, keepdims=False)
+    loss_local = scale * jnp.sum(fault * fault)
+    mine = lax.dynamic_index_in_dim(jnp.stack(adjoints[::-1]), net, keepdims=False)
+    mine = lax.dynamic_index_in_dim(mine, core, keepdims=False)[:, None]
+
+    def columns(left, right):
+        left = left.T
+        blocks = jnp.split(right, nets, axis=1)
+        return jnp.stack(
+            [jnp.dot(left, block, preferred_element_type=f32).astype(bf16) for block in blocks]
+        )
+
+    grad_third = columns(hidden_second, (mine * inc).astype(bf16))
     grad_second = jnp.dot(
         hidden_first.T, (mine * slope_second).astype(bf16), preferred_element_type=f32
-    )
-    grad_first = jnp.dot(inputs.T, (mine * slope_first).astype(bf16), preferred_element_type=f32)
-
-    def columns(grad):
-        part = lax.psum_scatter(grad.astype(bf16), "batch", scatter_dimension=0, tiled=True)
-        part = jnp.transpose(part.reshape(part.shape[0], nets, -1), (1, 0, 2))
-        return lax.all_gather(swap(part), "batch", axis=1, tiled=True)
-
-    def lines(grad):
-        grad = grad.astype(bf16).reshape(nets, -1, grad.shape[1])
-        part = lax.psum_scatter(grad, "batch", scatter_dimension=1, tiled=True)
-        return lax.all_gather(swap(part), "batch", axis=1, tiled=True)
-
-    loss, grad_y, grad_z = lax.psum((loss_local, grad_y_part, grad_z_part), "batch")
-    return (
-        loss,
-        grad_y,
-        grad_z,
-        columns(grad_first),
-        lines(grad_second),
-        columns(grad_third),
-    )
+    ).astype(bf16)
+    grad_first = columns(inputs, (mine * slope_first).astype(bf16))
+    small = jnp.zeros((8, share), f32)
+    small = small.at[0].set(grad_z_part).at[1].set(loss_local).at[2].set(grad_y_part)
+    grad_first, grad_second, grad_third, small = reduce_grads(
+        (grad_first, grad_second.reshape(nets, -1, hidden), grad_third), small, rows
+    )
+    return small[1, 0], small[2, 0], small[0], grad_first, grad_second, grad_third
 
 
 def pick(mesh):
     def run(*args):
         nets = args[6].shape[0]
-        fits = mesh.shape["dim"] == nets
+        rows = mesh.shape["batch"]
+        fits = mesh.shape["dim"] == nets == PAIR * PAIR and rows == PAIR * PAIR * PAIR
         return (local_nets if fits else local_dense)(*args)
 
     return run

time: 523 us -> 217 us (0.41)
  waiting for transfers between devices: 352 us -> 0 us
  Pallas kernels: 0 us -> 181 us
  blocking collectives: 101 us -> 0 us
  between operations: 15.7 us -> 2.32 us
  starting transfers between devices: 11.9 us -> 0 us
  local copies, waits for them, and re-layouts: 20.5 us -> 11.5 us
    reduce_scatter x3 -> x0, waiting for transfers between devices: 186 us -> none  [the longest x2 124 us: columns(): lax.psum_scatter(grad.astype(bf16), 'batch', scatter_dimension=0, tiled=T...]
    pallas_call x0 -> x3, Pallas kernels: none -> 181 us  [the longest x1 126 us: reduce_grads(): pl.pallas_call(functools.partial(reduce_kernel, rows, nets), out_shape=tu...]
    all_gather x3 -> x0, waiting for transfers between devices: 118 us -> none  [the longest x2 68 us: columns(): return lax.all_gather(swap(part), 'batch', axis=1, tiled=True)]
    all_to_all x5 -> x0, blocking collectives: 75.9 us -> none  [swap(): return lax.all_to_all(value, 'dim', split_axis=0, concat_axis=0, tiled=True)]
    all_to_all x3 -> x0, waiting for transfers between devices: 48.5 us -> none  [swap(): return lax.all_to_all(value, 'dim', split_axis=0, concat_axis=0, tiled=True)]
    psum x1 -> x0, blocking collectives: 20.2 us -> none  [local_nets(): lax.psum((loss_local, grad_y_part, grad_z_part), 'batch')]
    all_to_all x3 -> x0, starting transfers between devices: 11.6 us -> none  [swap(): return lax.all_to_all(value, 'dim', split_axis=0, concat_axis=0, tiled=True)]
    unnamed x43 -> x24, local copies, waits for them, and re-layouts: 16.4 us -> 6.66 us
  transfers between devices with their start and end apart: 9 -> 0, of which waited for: 9 -> 0; matrix products, arithmetic and copies ran while one was open for 3% -> 0% of each run, Pallas kernels for 0% -> 0%
where the time goes in v3:
time: 217 us; the launch traced here: 216 us
  Pallas kernels  181 us (83%)
  matrix products  13 us (6%)
  local copies, waits for them, and re-layouts  11.5 us (5%)
  other arithmetic  8.84 us (4%)
  between operations  2.32 us (1%)
    pallas_call x1, Pallas kernels, reduce_grads(): pl.pallas_call(functools.partial(reduce_kernel, rows, nets), out_shape=tu...  126 us
    pallas_call x1, Pallas kernels, fetch(): pl.pallas_call(fetch_kernel, out_shape=(jax.ShapeDtypeStruct((paths, widt...  48.6 us
    unnamed x24, local copies, waits for them, and re-layouts  6.66 us
    pallas_call x1, Pallas kernels, share_level(): pl.pallas_call(share_kernel, out_shape=jax.ShapeDtypeStruct(shape, block....  6.18 us

profile of v3, /device:TPU:0, one launch (start us, length us, event | category | flops | bytes accessed | tf_op | source)
XLA Modules:
  0.0 216.3 jit_solution(8410826406029964160)
XLA Ops:
  1.3 0.7 convert_element_type.96
  2.0 1.7 fusion.13
  3.7 1.1 fusion.57
  4.9 1.3 fusion.34
  6.2 1.4 slice.173.inc
  7.6 48.6 %fetch.1 = (f32[256,1024]{1,0:T(8,128)S(1)}, bf16[256,1024]{1,0:T(8,128)(2,1)S(1)}, bf16[1024,1024]{1,0:T(8,128)(2,1)S(1)}, bf16[1024,1024]{1,0:T(8,128)(2,1)S(1)}, bf16[1024,1024]{1,0:T(8,128)(2,1)S(1)}) custom-call(f32[4,256,256]{2,1,0:T(8,128)S(1)} %slice.173.inc, bf16[4,256,256]{2,1,0:T(8,128)(2,1)S(1)} %pad_maximum_fusion.2.state, ...), custom_call_target="tpu_custom_call" | custom-call | tf_op jit(solution)/shard_map/fetch/pallas_call | solution.py:270
  56.2 0.7 convolution_tanh_fusion.1
  56.9 0.7 convolution_tanh_fusion
  57.7 0.8 fusion.19
  58.5 1.8 multiply_reduce_fusion
  60.4 0.6 copy-done.9
  61.0 6.2 %share_level.1 = f32[2,4,8,256]{3,2,1,0:T(8,128)} custom-call(f32[8,256]{1,0:T(8,128)} %copy-done.9), custom_call_target="tpu_custom_call" | custom-call | tf_op jit(solution)/shard_map/share_level/pallas_call | solution.py:308
  67.2 0.7 slice.179
  67.9 0.9 slice_reduce_fusion.1
  68.9 0.8 fusion.59
  69.8 0.6 multiply_reduce_fusion.2
  71.1 3.9 %fusion.1 = bf16[256,1024]{1,0:T(8,128)(2,1)} fusion(bf16[1024,1024]{1,0:T(8,128)(2,1)} %copy-done, f32[256,1024]{1,0:T(8,128)S(1)} %convolution_tanh_fusion.1, f32[256]{0:T(256)S(1)} %bitcast.160, f32[256,1024]{1,0:T(8,128)} %get-tuple-element.140, f32[256,1024]{1,0:T(8,128)} %copy-done.5), kind=kOutput, calls=%fused_computation.8 | convolution fusion | flops 539230208 | bytes 5768192 | tf_op jit(solution)/shard_map/dot_general | solution.py:543
  75.0 2.2 %convolution_convert_fusion = bf16[1024,1024]{1,0:T(8,128)(2,1)} fusion(f32[256]{0:T(256)S(1)} %bitcast.161, f32[256,1024]{1,0:T(8,128)S(1)} %copy-done.7, f32[256,1024]{1,0:T(8,128)S(1)} %copy-done.6, f32[256,1024]{1,0:T(8,128)S(1)} %convolution_tanh_fusion.1), kind=kOutput, calls=%fused_computation.2 | convolution fusion | flops 539492352 | bytes 5243904 | tf_op jit(solution)/shard_map/dot_general | solution.py:585
  77.4 0.6 multiply_reduce_fusion.1
  78.0 1.1 fusion.17
  79.0 0.7 broadcast.196
  80.2 0.4 fusion.8
  80.5 0.4 fusion.7
  80.9 0.4 fusion.6
  81.5 0.8 copy-done.8
  84.0 1.3 copy-done.1
  85.3 125.9 %reduce_grads.1 = (bf16[4,1024,256]{2,1,0:T(8,128)(2,1)S(1)}, bf16[4,256,1024]{2,1,0:T(8,128)(2,1)S(1)}, bf16[4,1024,256]{2,1,0:T(8,128)(2,1)S(1)}, f32[8,256]{1,0:T(8,128)S(1)}) custom-call(bf16[4,1024,256]{2,1,0:T(8,128)(2,1)S(1)} %pad_maximum_fusion.refs_0_, bf16[4,256,1024]{2,1,0:T(8,128)(2,1)S(1)} %bitcast.159, ...), custom_call_target="tpu_custom_call" | custom-call | tf_op jit(solution)/shard_map/reduce_grads/pallas_call | solution.py:479
  211.3 0.6 slice.193
  211.9 0.5 fusion.61
  212.4 1.3 copy.47
  213.7 1.3 copy.48
  215.0 1.3 copy.49
  (41 shorter events, 2.9 us)
Async XLA Ops:
  2.0 5.6 %copy-start.4 = (bf16[4,256,1024]{2,1,0:T(8,128)(2,1)S(1)}, bf16[4,256,1024]{2,1,0:T(8,128)(2,1)}, u32[]{:S(2)}) copy-start(bf16[4,256,1024]{2,1,0:T(8,128)(2,1)} %second.1) | copy-start | bytes 6291460
  4.8 2.7 %copy-start.2 = (bf16[4,1024,256]{2,1,0:T(8,128)(2,1)S(1)}, bf16[4,1024,256]{2,1,0:T(8,128)(2,1)}, u32[]{:S(2)}) copy-start(bf16[4,1024,256]{2,1,0:T(8,128)(2,1)} %third.1) | copy-start | bytes 6291460
  4.8 2.7 %copy-start.3 = (bf16[4,1024,256]{2,1,0:T(8,128)(2,1)S(1)}, bf16[4,1024,256]{2,1,0:T(8,128)(2,1)}, u32[]{:S(2)}) copy-start(bf16[4,1024,256]{2,1,0:T(8,128)(2,1)} %first.1) | copy-start | bytes 6291460
  56.2 1.5 copy-start
  57.7 2.6 %copy-start.5 = (f32[256,1024]{1,0:T(8,128)}, f32[256,1024]{1,0:T(8,128)S(1)}, u32[]{:S(2)}) copy-start(f32[256,1024]{1,0:T(8,128)S(1)} %convolution_tanh_fusion) | copy-start | bytes 3145732
  60.4 0.6 copy-start.9
  71.1 4.0 %copy-start.6 = (f32[256,1024]{1,0:T(8,128)S(1)}, f32[256,1024]{1,0:T(8,128)}, u32[]{:S(2)}) copy-start(f32[256,1024]{1,0:T(8,128)} %copy-done.5) | copy-start | bytes 3145732
  71.1 4.0 %copy-start.7 = (f32[256,1024]{1,0:T(8,128)S(1)}, f32[256,1024]{1,0:T(8,128)}, u32[]{:S(2)}) copy-start(f32[256,1024]{1,0:T(8,128)} %get-tuple-element.140) | copy-start | bytes 3145732
  81.3 1.0 copy-start.8
  83.7 1.6 copy-start.1

commit v4 on v3

--- a/solution.py
+++ b/solution.py
@@ -190,9 +190,6 @@
         return pltpu.make_async_copy(value.at[net], out.at[:, columns(me)], own_path.at[index])
 
     aligned = core == side
-    for index in range(2):
-        for up, ac in ((0, 1), (1, 1), (1, 0)):
-            path_copy(index, up, ac).start()
     chip_copies, waits = [], []
     for index, (value, out, lines) in enumerate(mats):
         cut = value.shape[1] // PAIR
@@ -202,6 +199,10 @@
         )
         copy.start()
         chip_copies.append(copy)
+
+    for index in range(2):
+        for up, ac in ((0, 1), (1, 1), (1, 0)):
+            path_copy(index, up, ac).start()
 
     @pl.when(aligned)
     def _():
@@ -318,7 +319,8 @@
 
 
 def reduce_kernel(rows, nets, *refs):
-    grads, small, outs, small_out = refs[0:3], refs[3], refs[4:7], refs[7]
+    lefts, rights, refs = refs[0:3], refs[3:6], refs[6:]
+    small, outs, small_out, grads = refs[0], refs[1:4], refs[4], refs[5:8]
     zero, one, two = refs[8:11], refs[11:14], refs[14:17]
     sent_one, sent_two, held = refs[17:20], refs[20:23], refs[23:26]
     gathered = refs[26]
@@ -353,6 +355,18 @@
 
     def core_step(index):
         mat, turn = chunks[index]
+        for part in range(PAIR):
+            shard = flip(chip, turn) * PAIR + part
+            depth, width = grads[mat].shape[1:]
+            left, right = lefts[mat][...], rights[mat]
+            if width == right.shape[1]:
+                left = lefts[mat][:, pl.ds(pl.multiple_of(shard * depth, depth), depth)]
+                right = right[...]
+            else:
+                right = right[:, pl.ds(pl.multiple_of(shard * width, width), width)]
+            grads[mat][shard] = lax.dot_general(
+                left, right, (((0,), (0,)), ((), ())), preferred_element_type=f32
+            ).astype(bf16)
         copy = remote(
             grads[mat].at[shards(turn), span(mat, (1 - core) * 4, 4), :],
             zero[mat].at[shards(turn)], zero_sems, index, partner,
@@ -434,19 +448,24 @@
         copies["back_far", index].wait_recv()
         spread(index, 2, (1 - low) * PAIR, PAIR)
 
-    for index in range(len(chunks)):
-        core_step(index)
     small_copies = []
     for jump in range(1, rows):
         copy = remote(small, gathered.at[row], small_sems, jump - 1, {"batch": lax.rem(row + jump, rows)})
         copy.start()
         small_copies.append(copy)
     gathered[row] = small[...]
-    stages = (low_step, high_step, final_step, gather_step, last_step)
-    for time in range(len(chunks) + len(stages) - 1):
-        for lag in reversed(range(len(stages))):
+    stages = (
+        (0, core_step),
+        (1, low_step),
+        (3, high_step),
+        (5, final_step),
+        (6, gather_step),
+        (8, last_step),
+    )
+    for time in range(len(chunks) + stages[-1][0]):
+        for lag, stage in reversed(stages):
             if 0 <= time - lag < len(chunks):
-                stages[lag](time - lag)
+                stage(time - lag)
     for copy in small_copies:
         copy.wait()
     summed = gathered[0]
@@ -460,8 +479,8 @@
             copy.wait_send()
 
 
-def reduce_grads(grads, small, rows):
-    nets = grads[0].shape[0]
+def reduce_grads(lefts, rights, small, shapes, rows):
+    nets = shapes[0][0]
     bf16 = jnp.bfloat16
     any_spec = pl.BlockSpec(memory_space=pl.ANY)
     vmem = pl.BlockSpec(memory_space=pltpu.VMEM)
@@ -469,8 +488,7 @@
 
     def pieces(count):
         return [
-            pltpu.VMEM((nets, count * (grad.shape[1] // rows), grad.shape[2]), bf16)
-            for grad in grads
+            pltpu.VMEM((nets, count * (shape[1] // rows), shape[2]), bf16) for shape in shapes
         ]
 
     def dma(count):
@@ -478,11 +496,12 @@
 
     return pl.pallas_call(
         functools.partial(reduce_kernel, rows, nets),
-        out_shape=tuple(jax.ShapeDtypeStruct(grad.shape, bf16) for grad in grads)
+        out_shape=tuple(jax.ShapeDtypeStruct(shape, bf16) for shape in shapes)
         + (jax.ShapeDtypeStruct(small.shape, small.dtype),),
-        in_specs=[vmem] * 4,
+        in_specs=[vmem] * 7,
         out_specs=(any_spec,) * 3 + (vmem,),
-        scratch_shapes=pieces(4)
+        scratch_shapes=pieces(rows)
+        + pieces(4)
         + pieces(2)
         + pieces(1)
         + pieces(2)
@@ -501,7 +520,7 @@
             collective_id=1, has_side_effects=True, vmem_limit_bytes=36 * 1024 * 1024
         ),
         name="reduce_grads",
-    )(*grads, small)
+    )(*lefts, *rights, small)
 
 
 def local_nets(
@@ -574,22 +593,15 @@
     mine = lax.dynamic_index_in_dim(jnp.stack(adjoints[::-1]), net, keepdims=False)
     mine = lax.dynamic_index_in_dim(mine, core, keepdims=False)[:, None]
 
-    def columns(left, right):
-        left = left.T
-        blocks = jnp.split(right, nets, axis=1)
-        return jnp.stack(
-            [jnp.dot(left, block, preferred_element_type=f32).astype(bf16) for block in blocks]
-        )
-
-    grad_third = columns(hidden_second, (mine * inc).astype(bf16))
-    grad_second = jnp.dot(
-        hidden_first.T, (mine * slope_second).astype(bf16), preferred_element_type=f32
-    ).astype(bf16)
-    grad_first = columns(inputs, (mine * slope_first).astype(bf16))
     small = jnp.zeros((8, share), f32)
     small = small.at[0].set(grad_z_part).at[1].set(loss_local).at[2].set(grad_y_part)
+    rights = tuple((mine * value).astype(bf16) for value in (slope_first, slope_second, inc))
     grad_first, grad_second, grad_third, small = reduce_grads(
-        (grad_first, grad_second.reshape(nets, -1, hidden), grad_third), small, rows
+        (inputs, hidden_first, hidden_second),
+        rights,
+        small,
+        (w_first.shape, w_second.shape, w_third.shape),
+        rows,
     )
     return small[1, 0], small[2, 0], small[0], grad_first, grad_second, grad_third
 

time: 217 us -> 205 us (0.945)
  Pallas kernels: 181 us -> 173 us
  matrix products: 13 us -> 5.89 us
    pallas_call x1, Pallas kernels: 48.6 us -> 38.8 us  [fetch(): pl.pallas_call(fetch_kernel, out_shape=(jax.ShapeDtypeStruct((paths, widt...]
    dot_general x9 -> x0, matrix products: 5.03 us -> none  [the longest x8 2.82 us: columns(): jnp.dot(left, block, preferred_element_type=f32).astype(bf16)]
    dot_general x1, matrix products: 3.94 us -> 0.85 us  [local_nets(): jnp.dot(slope_second.astype(bf16), second.T, preferred_element_type=f32)]
    unnamed x24 -> x40, local copies, waits for them, and re-layouts: 6.66 us -> 8.18 us
where the time goes in v4:
time: 205 us; the launch traced here: 202 us
  Pallas kernels  173 us (84%)
  local copies, waits for them, and re-layouts  13 us (6%)
  other arithmetic  7.99 us (4%)
  matrix products  5.89 us (3%)
  between operations  2.26 us (1%)
    pallas_call x1, Pallas kernels, reduce_grads(): pl.pallas_call(functools.partial(reduce_kernel, rows, nets), out_shape=tu...  127 us
    pallas_call x1, Pallas kernels, fetch(): pl.pallas_call(fetch_kernel, out_shape=(jax.ShapeDtypeStruct((paths, widt...  38.8 us
    unnamed x40, local copies, waits for them, and re-layouts  8.18 us
    pallas_call x1, Pallas kernels, share_level(): pl.pallas_call(share_kernel, out_shape=jax.ShapeDtypeStruct(shape, block....  7.18 us

profile of v4, /device:TPU:0, one launch (start us, length us, event | category | flops | bytes accessed | tf_op | source)
XLA Modules:
  0.0 202.3 jit_solution(7470852610168429808)
XLA Ops:
  0.6 1.1 fusion.37
  1.8 1.3 fusion.15
  3.1 1.4 slice.173.inc
  4.5 1.6 copy-done.5
  6.1 38.8 %fetch.1 = (f32[256,1024]{1,0:T(8,128)S(1)}, bf16[256,1024]{1,0:T(8,128)(2,1)S(1)}, bf16[1024,1024]{1,0:T(8,128)(2,1)S(1)}, bf16[1024,1024]{1,0:T(8,128)(2,1)S(1)}, bf16[1024,1024]{1,0:T(8,128)(2,1)S(1)}) custom-call(f32[4,256,256]{2,1,0:T(8,128)S(1)} %slice.173.inc, bf16[4,256,256]{2,1,0:T(8,128)(2,1)S(1)} %pad_maximum_fusion.state, ...), custom_call_target="tpu_custom_call" | custom-call | tf_op jit(solution)/shard_map/fetch/pallas_call | solution.py:271
  44.9 1.7 fusion.42
  46.6 0.7 convolution_tanh_fusion
  47.3 0.8 copy-done
  48.1 0.8 fusion.10
  48.9 0.2 copy-done.8
  49.1 1.8 multiply_reduce_fusion
  51.0 0.3 fusion.4
  51.4 0.6 copy-done.13
  52.0 7.2 %share_level.1 = f32[2,4,8,256]{3,2,1,0:T(8,128)} custom-call(f32[8,256]{1,0:T(8,128)} %copy-done.13), custom_call_target="tpu_custom_call" | custom-call | tf_op jit(solution)/shard_map/share_level/pallas_call | solution.py:309
  59.2 0.8 fusion.39
  60.0 0.9 slice_reduce_fusion.1
  60.9 0.7 slice.179
  62.5 0.6 multiply_reduce_fusion.2
  63.1 0.6 multiply_reduce_fusion.1
  63.7 0.6 broadcast.196
  64.3 1.1 fusion.8
  66.2 1.9 multiply_convert_fusion
  68.1 0.2 copy-done.11
  68.3 0.3 copy-done.12
  68.7 0.9 fusion.1.refs_3_
  69.5 0.2 copy-done.1
  70.0 127.2 %reduce_grads.1 = (bf16[4,1024,256]{2,1,0:T(8,128)(2,1)S(1)}, bf16[4,256,1024]{2,1,0:T(8,128)(2,1)S(1)}, bf16[4,1024,256]{2,1,0:T(8,128)(2,1)S(1)}, f32[8,256]{1,0:T(8,128)S(1)}) custom-call(bf16[256,1024]{1,0:T(8,128)(2,1)S(1)} %copy-done.7, bf16[256,1024]{1,0:T(8,128)(2,1)S(1)} %copy-done.1, bf16[256,1024]{1,0:T(8,128)(2,1)S(1)} %copy-done.2, ...), custom_call_target="tpu_custom_call" | custom-call | tf_op jit(solution)/shard_map/reduce_grads/pallas_call | solution.py:497
  197.2 0.5 fusion.41
  197.7 0.6 slice.193
  198.3 1.3 copy.47
  199.6 1.3 copy.48
  200.9 1.3 copy.49
  (46 shorter events, 0.8 us)
Async XLA Ops:
  1.7 2.7 %copy-start.3 = (bf16[4,1024,256]{2,1,0:T(8,128)(2,1)S(1)}, bf16[4,1024,256]{2,1,0:T(8,128)(2,1)}, u32[]{:S(2)}) copy-start(bf16[4,1024,256]{2,1,0:T(8,128)(2,1)} %third.1) | copy-start | bytes 6291460
  1.8 2.7 %copy-start.4 = (bf16[4,1024,256]{2,1,0:T(8,128)(2,1)S(1)}, bf16[4,1024,256]{2,1,0:T(8,128)(2,1)}, u32[]{:S(2)}) copy-start(bf16[4,1024,256]{2,1,0:T(8,128)(2,1)} %first.1) | copy-start | bytes 6291460
  4.5 1.6 copy-start.5
  44.9 1.7 copy-start.6
  47.3 0.8 copy-start
  48.1 1.0 copy-start.8
  49.1 1.9 copy-start.10
  49.1 1.9 copy-start.14
  49.1 1.9 copy-start.16
  49.1 1.9 copy-start.17
  49.1 2.3 %copy-start.15 = (s32[256]{0:T(256)S(1)}, s32[256]{0:T(256)}, u32[]{:S(2)}) copy-start(s32[256]{0:T(256)} %param.27) | copy-start | bytes 3076
  51.4 0.6 copy-start.13
  66.2 2.0 copy-start.9
  66.2 2.2 %copy-start.11 = (f32[256,1024]{1,0:T(8,128)S(1)}, f32[256,1024]{1,0:T(8,128)}, u32[]{:S(2)}) copy-start(f32[256,1024]{1,0:T(8,128)} %get-tuple-element.144) | copy-start | bytes 3145732
  66.2 2.5 %copy-start.12 = (f32[256,1024]{1,0:T(8,128)S(1)}, f32[256,1024]{1,0:T(8,128)}, u32[]{:S(2)}) copy-start(f32[256,1024]{1,0:T(8,128)} %get-tuple-element.143) | copy-start | bytes 3145732
  68.7 1.0 copy-start.1
  68.7 1.2 copy-start.2
  68.7 1.4 copy-start.7
